TPU v7x, 32 devices: a whole 2x2x4 slice. The times are simulated.
32 devices in a mesh: fsdp: 16 (over z, y, x), tensor: 2 (over core).
Axes of the slice: x: 2, y: 2, z: 4, core: 2. Of those that a mesh axis runs over, the one named last changes fastest.
Arguments:
- images: bfloat16 [16, 577, 1024], P('fsdp'), may hold values from -6 to 6
- out_cotangent: bfloat16 [16, 577, 1024], P('fsdp'), may hold values from -6 to 6
- qkv_weight: bfloat16 [1024, 3, 1024], P('fsdp', None, 'tensor'), may hold values from -0.1875 to 0.1875
- out_weight: bfloat16 [1024, 1024], P('fsdp', 'tensor'), may hold values from -1.5 to 1.5
- up_weight: bfloat16 [1024, 4096], P('fsdp', 'tensor'), may hold values from -0.1875 to 0.1875
- down_weight: bfloat16 [1024, 4096], P('fsdp', 'tensor'), may hold values from -0.09375 to 0.09375
- norm_gain: float32 [2, 1024], replicated, may hold values from 0.1 to 1.9
- norm_bias: float32 [2, 1024], replicated, may hold values from -2 to 2
- attn_bias: float32 [2, 1024], P(None, 'tensor'), may hold values from -2 to 2
- res_bias: float32 [2, 1024], replicated, may hold values from -2 to 2
- up_bias: float32 [4096], P('tensor'), may hold values from -2 to 2
- qkv_moment: float32 [1024, 3, 1024], P('fsdp', None, 'tensor'), may hold values from -512 to 512
- out_moment: float32 [1024, 1024], P('fsdp', 'tensor'), may hold values from -512 to 512
- up_moment: float32 [1024, 4096], P('fsdp', 'tensor'), may hold values from -512 to 512
- down_moment: float32 [1024, 4096], P('fsdp', 'tensor'), may hold values from -512 to 512
- gain_moment: float32 [2, 1024], replicated, may hold values from -512 to 512
- nbias_moment: float32 [2, 1024], replicated, may hold values from -512 to 512
- abias_moment: float32 [2, 1024], P(None, 'tensor'), may hold values from -512 to 512
- rbias_moment: float32 [2, 1024], replicated, may hold values from -512 to 512
- ubias_moment: float32 [4096], P('tensor'), may hold values from -512 to 512
Outputs:
- block_out: bfloat16 [16, 577, 1024], P('fsdp')
- images_grad: float32 [16, 577, 1024], P('fsdp')
- qkv_weight_grad: float32 [1024, 3, 1024], P('fsdp', None, 'tensor')
- out_weight_grad: float32 [1024, 1024], P('fsdp', 'tensor')
- up_weight_grad: float32 [1024, 4096], P('fsdp', 'tensor')
- down_weight_grad: float32 [1024, 4096], P('fsdp', 'tensor')
- norm_gain_grad: float32 [2, 1024], replicated
- norm_bias_grad: float32 [2, 1024], replicated
- attn_bias_grad: float32 [2, 1024], P(None, 'tensor')
- res_bias_grad: float32 [2, 1024], replicated
- up_bias_grad: float32 [4096], P('tensor')
- qkv_weight_new: float32 [1024, 3, 1024], P('fsdp', None, 'tensor')
- out_weight_new: float32 [1024, 1024], P('fsdp', 'tensor')
- up_weight_new: float32 [1024, 4096], P('fsdp', 'tensor')
- down_weight_new: float32 [1024, 4096], P('fsdp', 'tensor')
- norm_gain_new: float32 [2, 1024], replicated
- norm_bias_new: float32 [2, 1024], replicated
- attn_bias_new: float32 [2, 1024], P(None, 'tensor')
- res_bias_new: float32 [2, 1024], replicated
- up_bias_new: float32 [4096], P('tensor')
- qkv_moment_new: float32 [1024, 3, 1024], P('fsdp', None, 'tensor')
- out_moment_new: float32 [1024, 1024], P('fsdp', 'tensor')
- up_moment_new: float32 [1024, 4096], P('fsdp', 'tensor')
- down_moment_new: float32 [1024, 4096], P('fsdp', 'tensor')
- gain_moment_new: float32 [2, 1024], replicated
- nbias_moment_new: float32 [2, 1024], replicated
- abias_moment_new: float32 [2, 1024], P(None, 'tensor')
- rbias_moment_new: float32 [2, 1024], replicated
- ubias_moment_new: float32 [4096], P('tensor')
All inputs are finite; a program needn't handle non-finite values.
Results may differ from a plain program's by a relative error of at most 0.013.
Values may be sent and summed in bfloat16 or wider, within the bound.
No kernel may reach another device: no remote copies, remote signals or barrier semaphores. Data moves between devices by JAX's collectives and lax.ppermute only.
A program may use at most 256 MiB of HBM per device.

v0:
```python
import math

import jax
import jax.numpy as jnp
from jax import lax
from jax.sharding import PartitionSpec as P

HEAD_DIM = 64
NS_STEPS = 5


HIGHEST = lax.Precision.HIGHEST
LN_EPS = 1e-06
NS_EPS = 1e-06
COEF_A = 3.4445
COEF_B = -4.775
COEF_C = 2.0315
MOMENTUM = 0.95
MUON_RATE = 0.15
VECTOR_RATE = 0.002
ROOT_HALF = 0.7071067811865476
ROOT_TWO_PI = 2.5066282746310002


def for_sending(array):
    return jax.tree.map(lambda a: a.astype(jnp.bfloat16) if a.dtype == jnp.float32 else a, array)


def spread(block, axis, source):
    block = jnp.where(lax.axis_index(axis) == source, block, jnp.zeros_like(block))
    return lax.psum(block, axis)


def gelu_value(upper):
    return 0.5 * upper * (1.0 + jax.scipy.special.erf(upper * ROOT_HALF))


def gelu_slope(upper):
    return (
        0.5 * (1.0 + jax.scipy.special.erf(upper * ROOT_HALF))
        + upper * jnp.exp(-0.5 * upper * upper) / ROOT_TWO_PI
    )


def layer_stats(values):
    center = values - jnp.mean(values, axis=-1, keepdims=True)
    inverse = lax.rsqrt(jnp.mean(center * center, axis=-1, keepdims=True) + LN_EPS)
    return (center * inverse, inverse)


def norm_back(grad_out, normed, inverse, gain):
    scaled = grad_out * gain
    return inverse * (
        scaled
        - jnp.mean(scaled, axis=-1, keepdims=True)
        - normed * jnp.mean(scaled * normed, axis=-1, keepdims=True)
    )


def orthogonal(matrix):
    rows, cols = matrix.shape
    current = matrix.astype(jnp.float32)
    if rows > cols:
        current = current.T
    norm_value = jnp.sqrt(jnp.sum(current * current))
    current = current / (norm_value + NS_EPS)
    for repeat in range(NS_STEPS):
        gram = jnp.dot(current, current.T, precision=HIGHEST)
        poly = COEF_B * gram + COEF_C * jnp.dot(gram, gram, precision=HIGHEST)
        current = COEF_A * current + jnp.dot(poly, current, precision=HIGHEST)
    if rows > cols:
        current = current.T
    return current


def zero_float(matrix):
    return jnp.zeros(matrix.shape, jnp.float32)


def split_heads(block):
    return block.reshape(block.shape[0], 3, -1, HEAD_DIM)


def attend(block):
    parts = split_heads(block)
    scale = HEAD_DIM ** (-0.5)
    scores = (
        jnp.einsum("qhe,khe->hqk", parts[:, 0], parts[:, 1], preferred_element_type=jnp.float32)
        * scale
    )
    ceiling = jnp.max(scores, axis=-1, keepdims=True)
    exponent = jnp.exp(scores - ceiling)
    total = jnp.sum(exponent, axis=-1, keepdims=True)
    probs = exponent / total
    mixed = jnp.einsum(
        "hqk,khe->qhe", probs.astype(jnp.bfloat16), parts[:, 2], preferred_element_type=jnp.float32
    )
    return (mixed.reshape(block.shape[0], -1).astype(jnp.bfloat16), ceiling + jnp.log(total))


def attend_back(items):
    block, log_total, mixed_grad = items
    parts = split_heads(block)
    scale = HEAD_DIM ** (-0.5)
    query_part = parts[:, 0]
    key_part = parts[:, 1]
    value_part = parts[:, 2]
    scores = (
        jnp.einsum("qhe,khe->hqk", query_part, key_part, preferred_element_type=jnp.float32) * scale
    )
    probs = jnp.exp(scores - log_total)
    heads_grad = mixed_grad.reshape(mixed_grad.shape[0], -1, HEAD_DIM)
    prob_grad = jnp.einsum(
        "qhe,khe->hqk", heads_grad, value_part, preferred_element_type=jnp.float32
    )
    value_grad = jnp.einsum(
        "hqk,qhe->khe", probs.astype(jnp.bfloat16), heads_grad, preferred_element_type=jnp.float32
    )
    score_grad = (probs * (prob_grad - jnp.sum(probs * prob_grad, axis=-1, keepdims=True))).astype(
        jnp.bfloat16
    )
    query_grad = (
        jnp.einsum("hqk,khe->qhe", score_grad, key_part, preferred_element_type=jnp.float32) * scale
    )
    key_grad = (
        jnp.einsum("hqk,qhe->khe", score_grad, query_part, preferred_element_type=jnp.float32)
        * scale
    )
    stacked = jnp.stack([query_grad, key_grad, value_grad], axis=1)
    return stacked.reshape(block.shape[0], 3, -1).astype(jnp.bfloat16)


def tensor_total(partial_sum):
    return lax.psum(partial_sum, "tensor")


def pick_owned(matrices, marks, rank):
    chosen = jnp.zeros_like(matrices[0])
    for matrix, mark in zip(matrices, marks):
        chosen = jnp.where(rank == mark, matrix, chosen)
    return chosen


def body(
    images,
    out_cotangent,
    qkv_weight,
    out_weight,
    up_weight,
    down_weight,
    norm_gain,
    norm_bias,
    attn_bias,
    res_bias,
    up_bias,
    qkv_moment,
    out_moment,
    up_moment,
    down_moment,
    gain_moment,
    nbias_moment,
    abias_moment,
    rbias_moment,
    ubias_moment,
):
    rank = lax.axis_index("fsdp")
    fsdp_count = lax.axis_size("fsdp")
    owner_list = [index * fsdp_count // 6 for index in range(6)]
    shard_rows = qkv_weight.shape[0]
    qkv_full, out_full, up_full, down_full = (
        lax.all_gather(qkv_weight, "fsdp", axis=0, tiled=True),
        lax.all_gather(out_weight, "fsdp", axis=0, tiled=True),
        lax.all_gather(up_weight, "fsdp", axis=0, tiled=True),
        lax.all_gather(down_weight, "fsdp", axis=0, tiled=True),
    )
    image_count, length, width = images.shape
    head_width = qkv_full.shape[2]
    tokens = images.reshape(-1, width).astype(jnp.float32)
    hat_one, inv_one = layer_stats(tokens)
    normed1 = (hat_one * norm_gain[0] + norm_bias[0]).astype(jnp.bfloat16)
    proj = jnp.einsum("td,djh->tjh", normed1, qkv_full, preferred_element_type=jnp.float32)
    bias_three = jnp.stack([attn_bias[0], jnp.zeros_like(attn_bias[0]), attn_bias[1]])
    proj = (proj + bias_three).astype(jnp.bfloat16)
    proj_images = proj.reshape(image_count, length, 3, head_width)
    attn_images, log_totals = lax.map(attend, proj_images)
    attn_rows = attn_images.reshape(-1, head_width)
    branch = tensor_total(
        jnp.einsum("th,dh->td", attn_rows, out_full, preferred_element_type=jnp.float32)
    )
    mid = tokens + branch + res_bias[0]
    hat_two, inv_two = layer_stats(mid)
    normed2 = (hat_two * norm_gain[1] + norm_bias[1]).astype(jnp.bfloat16)
    upper = jnp.dot(normed2, up_full, preferred_element_type=jnp.float32) + up_bias
    hidden = gelu_value(upper).astype(jnp.bfloat16)
    second = tensor_total(
        jnp.einsum("tf,df->td", hidden, down_full, preferred_element_type=jnp.float32)
    )
    result = mid + second + res_bias[1]
    grad_top = out_cotangent.reshape(-1, width).astype(jnp.float32)
    top_low = grad_top.astype(jnp.bfloat16)
    downw_grad = jnp.einsum("td,tf->df", top_low, hidden, preferred_element_type=jnp.float32)
    hidden_grad = jnp.dot(top_low, down_full, preferred_element_type=jnp.float32)
    upper_grad = (hidden_grad * gelu_slope(upper)).astype(jnp.bfloat16)
    ubias_grad = jnp.sum(upper_grad, axis=0, dtype=jnp.float32)
    upw_grad = jnp.einsum("td,tf->df", normed2, upper_grad, preferred_element_type=jnp.float32)
    normed2_grad = tensor_total(
        jnp.einsum("tf,df->td", upper_grad, up_full, preferred_element_type=jnp.float32)
    )
    gain_two = jnp.sum(normed2_grad * hat_two, axis=0)
    shift_two = jnp.sum(normed2_grad, axis=0)
    mid_grad = grad_top + norm_back(normed2_grad, hat_two, inv_two, norm_gain[1])
    rbias_grad = jnp.stack([jnp.sum(mid_grad, axis=0), jnp.sum(grad_top, axis=0)])
    mid_low = mid_grad.astype(jnp.bfloat16)
    outw_grad = jnp.einsum("td,th->dh", mid_low, attn_rows, preferred_element_type=jnp.float32)
    attn_grad = jnp.dot(mid_low, out_full, preferred_element_type=jnp.float32).astype(jnp.bfloat16)
    proj_grad = lax.map(
        attend_back, (proj_images, log_totals, attn_grad.reshape(image_count, length, head_width))
    )
    proj_grad = proj_grad.reshape(-1, 3, head_width)
    qkv_grad = jnp.einsum("td,tjh->djh", normed1, proj_grad, preferred_element_type=jnp.float32)
    abias_grad = jnp.stack(
        [
            jnp.sum(proj_grad[:, 0], axis=0, dtype=jnp.float32),
            jnp.sum(proj_grad[:, 2], axis=0, dtype=jnp.float32),
        ]
    )
    normed1_grad = tensor_total(
        jnp.einsum("tjh,djh->td", proj_grad, qkv_full, preferred_element_type=jnp.float32)
    )
    gain_one = jnp.sum(normed1_grad * hat_one, axis=0)
    shift_one = jnp.sum(normed1_grad, axis=0)
    input_grad = mid_grad + norm_back(normed1_grad, hat_one, inv_one, norm_gain[0])
    gain_grad = jnp.stack([gain_one, gain_two])
    nbias_grad = jnp.stack([shift_one, shift_two])
    grad_shards = (
        lax.psum_scatter(qkv_grad, "fsdp", scatter_dimension=0, tiled=True),
        lax.psum_scatter(outw_grad, "fsdp", scatter_dimension=0, tiled=True),
        lax.psum_scatter(upw_grad, "fsdp", scatter_dimension=0, tiled=True),
        lax.psum_scatter(downw_grad, "fsdp", scatter_dimension=0, tiled=True),
    )
    vector_grads = lax.psum((gain_grad, nbias_grad, abias_grad, rbias_grad, ubias_grad), "fsdp")
    moment_shards = tuple(
        (
            MOMENTUM * stored + gradient
            for stored, gradient in zip(
                (qkv_moment, out_moment, up_moment, down_moment), grad_shards
            )
        )
    )
    shard_low = tuple((stored.astype(jnp.bfloat16) for stored in moment_shards))
    weight_shards = [
        qkv_weight[:, 0],
        qkv_weight[:, 1],
        qkv_weight[:, 2],
        out_weight,
        up_weight,
        down_weight,
    ]
    owns_narrow = jnp.any(jnp.array(owner_list[:4], jnp.int32) == rank)
    owns_wide = jnp.any(jnp.array(owner_list[4:], jnp.int32) == rank)
    low_moments = jax.tree.map(
        lambda part, own: part.astype(own.dtype),
        lax.all_gather(for_sending(shard_low), "fsdp", axis=0, tiled=True),
        shard_low,
    )
    matrices = [
        low_moments[0][:, 0],
        low_moments[0][:, 1],
        low_moments[0][:, 2],
        low_moments[1],
        low_moments[2],
        low_moments[3],
    ]
    narrow_pick = pick_owned(matrices[:4], owner_list[:4], rank)
    wide_pick = pick_owned(matrices[4:], owner_list[4:], rank)
    narrow_orth = lax.cond(owns_narrow, orthogonal, zero_float, narrow_pick)
    wide_orth = lax.cond(owns_wide, orthogonal, zero_float, wide_pick)
    updated = []
    for index in range(6):
        chosen = narrow_orth if index < 4 else wide_orth
        chosen = spread(chosen.astype(jnp.bfloat16), "fsdp", owner_list[index]).astype(chosen.dtype)
        piece = lax.dynamic_slice_in_dim(chosen, rank * shard_rows, shard_rows, 0)
        factor = 0.2 * math.sqrt(max(chosen.shape[0], chosen.shape[1]))
        updated.append(weight_shards[index].astype(jnp.float32) - MUON_RATE * (piece * factor))
    qkv_new = jnp.stack(updated[:3], axis=1)
    out_new = updated[3]
    up_new = updated[4]
    down_new = updated[5]
    vector_params = (norm_gain, norm_bias, attn_bias, res_bias, up_bias)
    vector_moments = (gain_moment, nbias_moment, abias_moment, rbias_moment, ubias_moment)
    vmoment_new = [
        MOMENTUM * stored + gradient for stored, gradient in zip(vector_moments, vector_grads)
    ]
    vparam_new = [param - VECTOR_RATE * stored for param, stored in zip(vector_params, vmoment_new)]
    block_out = result.reshape(image_count, length, width).astype(jnp.bfloat16)
    images_grad = input_grad.reshape(image_count, length, width)
    return (
        block_out,
        images_grad,
        grad_shards[0],
        grad_shards[1],
        grad_shards[2],
        grad_shards[3],
        vector_grads[0],
        vector_grads[1],
        vector_grads[2],
        vector_grads[3],
        vector_grads[4],
        qkv_new,
        out_new,
        up_new,
        down_new,
        vparam_new[0],
        vparam_new[1],
        vparam_new[2],
        vparam_new[3],
        vparam_new[4],
        moment_shards[0],
        moment_shards[1],
        moment_shards[2],
        moment_shards[3],
        vmoment_new[0],
        vmoment_new[1],
        vmoment_new[2],
        vmoment_new[3],
        vmoment_new[4],
    )


def solution(mesh):
    placed = (
        P("fsdp", None, None),
        P("fsdp", None, None),
        P("fsdp", None, "tensor"),
        P("fsdp", "tensor"),
        P("fsdp", "tensor"),
        P("fsdp", "tensor"),
        P(),
        P(),
        P(None, "tensor"),
        P(),
        P("tensor"),
        P("fsdp", None, "tensor"),
        P("fsdp", "tensor"),
        P("fsdp", "tensor"),
        P("fsdp", "tensor"),
        P(),
        P(),
        P(None, "tensor"),
        P(),
        P("tensor"),
    )
    return jax.shard_map(
        body,
        mesh=mesh,
        in_specs=placed,
        out_specs=(
            P("fsdp", None, None),
            P("fsdp", None, None),
            P("fsdp", None, "tensor"),
            P("fsdp", "tensor"),
            P("fsdp", "tensor"),
            P("fsdp", "tensor"),
            P(),
            P(),
            P(None, "tensor"),
            P(),
            P("tensor"),
            P("fsdp", None, "tensor"),
            P("fsdp", "tensor"),
            P("fsdp", "tensor"),
            P("fsdp", "tensor"),
            P(),
            P(),
            P(None, "tensor"),
            P(),
            P("tensor"),
            P("fsdp", None, "tensor"),
            P("fsdp", "tensor"),
            P("fsdp", "tensor"),
            P("fsdp", "tensor"),
            P(),
            P(),
            P(None, "tensor"),
            P(),
            P("tensor"),
        ),
        check_vma=False,
    )
```

profile of v0, /device:TPU:0, one launch (start us, length us, event | category | flops | bytes accessed | tf_op | source)
XLA Modules:
  0.0 1993.2 jit_solution(1661578997959915890)
XLA Ops:
  14.5 66.9 %all-gather.9.cloned.1.call-done = bf16[1024,3,512]{2,0,1:T(8,128)(2,1)} async-done(((bf16[64,3,512]{2,0,1:T(8,128)(2,1)}), bf16[1024,3,512]{2,0,1:T(8,128)(2,1)}) %all-gather.9.cloned.1.call-update) | async-done | bytes 3145744 | tf_op jit(solution)/shard_map/all_gather | solution.py:171
  81.4 5.4 add_convert_fusion.1
  86.8 2.7 copy.76
  89.6 2.1 multiply_reduce_fusion.1
  93.8 2.3 copy-done
  96.0 2.9 fusion.115
  98.9 39.0 %all-gather.11.cloned.1.call-done = bf16[1024,512]{1,0:T(8,128)(2,1)} async-done(((bf16[64,512]{1,0:T(8,128)(2,1)}), bf16[1024,512]{1,0:T(8,128)(2,1)}) %all-gather.11.cloned.1.call-update) | async-done | bytes 1048592 | tf_op jit(solution)/shard_map/all_gather | solution.py:172
  137.9 3.5 fusion.160
  143.5 18.8 all-reduce.8.cloned.1.call-done
  162.3 2.4 fusion.143
  165.1 76.6 %all-gather.13.cloned.1.call-done = bf16[1024,2048]{1,0:T(8,128)(2,1)} async-done(((bf16[64,2048]{1,0:T(8,128)(2,1)}), bf16[1024,2048]{1,0:T(8,128)(2,1)}) %all-gather.13.cloned.1.call-update) | async-done | bytes 4194320 | tf_op jit(solution)/shard_map/all_gather | solution.py:173
  241.7 7.7 multiply_convert_fusion.1
  249.4 69.2 %all-gather.15.cloned.1.call-done = bf16[1024,2048]{1,0:T(8,128)(2,1)} async-done(((bf16[64,2048]{1,0:T(8,128)(2,1)}), bf16[1024,2048]{1,0:T(8,128)(2,1)}) %all-gather.15.cloned.1.call-update) | async-done | bytes 4194320 | tf_op jit(solution)/shard_map/all_gather | solution.py:174
  318.6 7.6 convert_reduce_fusion
  327.6 4.1 fusion.162
  331.8 20.5 %all-reduce.10.cloned.1.call-done = f32[577,1024]{1,0:T(8,128)} async-done(((f32[577,1024]{1,0:T(8,128)}), f32[577,1024]{1,0:T(8,128)}) %all-reduce.10.cloned.1.call-update) | async-done | bytes 2363408 | tf_op jit(solution)/shard_map/psum | solution.py:134
  352.3 3.4 multiply_reduce_fusion.2
  358.9 2.4 fusion.121
  361.4 3.3 convolution_convert_fusion
  366.0 7.5 fusion.112
  373.5 2.1 copy.84
  375.6 7.5 multiply_reduce_fusion
  383.1 6.5 multiply_convert_fusion
  389.6 3.4 fusion.111
  394.1 4.1 fusion.110
  399.3 7.4 fusion.120
  406.8 7.7 fusion.135
  415.8 7.3 convolution_bitcast_fusion
  423.2 20.9 %reduce-scatter.7.cloned.1.call-done = f32[64,512]{1,0:T(8,128)} async-done(((f32[1024,512]{1,0:T(8,128)}), f32[64,512]{1,0:T(8,128)}) %reduce-scatter.7.cloned.1.call-update) | async-done | bytes 131088 | tf_op jit(solution)/shard_map/reduce_scatter | solution.py:237
  445.8 134.1 %reduce-scatter.5.cloned.1.call-done = f32[64,3,512]{2,0,1:T(8,128)} async-done(((f32[1024,3,512]{2,0,1:T(8,128)}), f32[64,3,512]{2,0,1:T(8,128)}) %reduce-scatter.5.cloned.1.call-update) | async-done | bytes 393232 | tf_op jit(solution)/shard_map/reduce_scatter | solution.py:236
  581.8 180.2 %reduce-scatter.9.cloned.1.call-done = f32[64,2048]{1,0:T(8,128)} async-done(((f32[1024,2048]{1,0:T(8,128)}), f32[64,2048]{1,0:T(8,128)}) %reduce-scatter.9.cloned.1.call-update) | async-done | bytes 524304 | tf_op jit(solution)/shard_map/reduce_scatter | solution.py:238
  764.0 181.0 %reduce-scatter.11.cloned.1.call-done = f32[64,2048]{1,0:T(8,128)} async-done(((f32[1024,2048]{1,0:T(8,128)}), f32[64,2048]{1,0:T(8,128)}) %reduce-scatter.11.cloned.1.call-update) | async-done | bytes 524304 | tf_op jit(solution)/shard_map/reduce_scatter | solution.py:239
  947.5 7.1 fusion.161
  954.6 3.5 convolution_bitcast_fusion.1
  961.3 44.5 %all-gather.19.cloned.1.call-done = bf16[1024,512]{1,0:T(8,128)(2,1)} async-done(((bf16[64,512]{1,0:T(8,128)(2,1)}), bf16[1024,512]{1,0:T(8,128)(2,1)}) %all-gather.19.cloned.1.call-update) | async-done | bytes 1048592 | tf_op jit(solution)/shard_map/all_gather | solution.py:263
  1005.9 69.9 %all-gather.17.cloned.1.call-done = bf16[1024,3,512]{2,0,1:T(8,128)(2,1)} async-done(((bf16[64,3,512]{2,0,1:T(8,128)(2,1)}), bf16[1024,3,512]{2,0,1:T(8,128)(2,1)}) %all-gather.17.cloned.1.call-update) | async-done | bytes 3145744 | tf_op jit(solution)/shard_map/all_gather | solution.py:263
  1076.2 66.7 %conditional.2 = (bf16[1024,512]{1,0:T(8,128)(2,1)}) conditional(s32[]{:T(128)} %convert_element_type.180, () %tuple.30, (pred[]{:T(512)}, pred[]{:T(512)}, bf16[1024,3,512]{2,0,1:T(8,128)(2,1)}, pred[1024,512]{1,0:T(8,128)(4,1)S(1)}, bf16[1024,512]{1,0:T(8,128)(2,1)S(1)}, /*index=5*/pred[1024,512]{1,0:T(8,128)(4,1)S(1)}, ...), branch_computations={%region_34.35_spmd, %region_35.37_spmd} | conditional | flops 40295464960 | bytes 97517640 | solution.py:276
  1076.2 2.3 copy.90
  1082.8 3.4 copy.86
  1086.2 4.2 fusion
  1091.1 5.3 fusion.20
  1098.4 3.6 fusion.19
  1102.0 4.2 fusion.24
  1108.1 3.9 multiply_add_fusion.2
  1112.0 3.5 fusion.158
  1117.4 4.0 fusion.159
  1121.5 3.7 fusion.22
  1127.1 3.6 fusion.21
  1130.8 4.2 fusion.16
  1136.9 4.5 fusion.3
  1142.9 3.3 broadcast_select_fusion.2
  1146.3 7.1 all-gather.21.cloned.1.call-done
  1153.4 76.8 %all-gather.23.cloned.1.call-done = bf16[1024,2048]{1,0:T(8,128)(2,1)} async-done(((bf16[64,2048]{1,0:T(8,128)(2,1)}), bf16[1024,2048]{1,0:T(8,128)(2,1)}) %all-gather.23.cloned.1.call-update) | async-done | bytes 4194320 | tf_op jit(solution)/shard_map/all_gather | solution.py:263
  1230.3 2.5 broadcast.162
  1232.8 8.4 conditional.3
  1232.8 2.6 broadcast.137
  1241.2 6.3 broadcast_select_fusion
  1249.3 11.1 all-reduce.12.cloned.1.call-done
  1260.4 3.1 fusion.107
  1263.5 2.4 fusion.106
  1266.2 3.8 copy.95
  1270.1 440.9 %all-reduce = (f32[2,1024]{1,0:T(2,128)S(1)}, f32[2,1024]{1,0:T(2,128)S(1)}, f32[2,512]{1,0:T(2,128)S(1)}, f32[2,1024]{1,0:T(2,128)S(1)}, f32[2048]{0:T(1024)S(1)}) all-reduce(f32[2,1024]{1,0:T(2,128)S(1)} %pad_maximum_fusion.5, f32[2,1024]{1,0:T(2,128)S(1)} %pad_maximum_fusion.6, ...), channel_id=1, replica_groups=mesh['fsdp'=16,'tensor'=2] {'fsdp'}, use_global_device_ids=true, to_apply=%region_21.22 | all-reduce | flops 9216 | bytes 73728 | tf_op jit(solution)/shard_map/psum | solution.py:241
  1714.1 3.3 fusion.116
  1717.5 261.8 %all-reduce.14.cloned.1.call-done = (bf16[1024,512]{1,0:T(8,128)(2,1)}, bf16[1024,512]{1,0:T(8,128)(2,1)}, bf16[1024,512]{1,0:T(8,128)(2,1)}, bf16[1024,512]{1,0...) async-done(((bf16[1024,512]{1,0:T(8,128)(2,1)}, bf16[1024,512]{1,0:T(8,128)(2,1)}, bf16[1024,512]{1,0:T(8,128)(2,1)}, bf16[1024,512]{1,0:T(8,128)(2,1)}, ...) | async-done | bytes 12582928 | tf_op jit(solution)/shard_map/psum | solution.py:31
  (213 shorter events, 58.7 us)
Async XLA Ops:
  7.2 74.2 %copy-start.6 = (bf16[1,577,1024]{2,1,0:T(8,128)(2,1)S(1)}, bf16[1,577,1024]{2,1,0:T(8,128)(2,1)}, u32[]{:S(2)}) copy-start(bf16[1,577,1024]{2,1,0:T(8,128)(2,1)} %param.26) | copy-start | bytes 3545092
  7.2 74.2 %all-gather.9.cloned.1.call-start = ((), (), s32[]{:S(2)}) async-start(), calls=%async_computation.4 | async-start | bytes 3342336 | tf_op jit(solution)/shard_map/all_gather | solution.py:171
  7.9 130.0 %all-gather.11.cloned.1.call-start = ((), (), s32[]{:S(2)}) async-start(), calls=%async_computation.5 | async-start | bytes 1114112 | tf_op jit(solution)/shard_map/all_gather | solution.py:172
  8.7 153.6 %all-reduce.8.cloned.1.call-start = ((), (), s32[]{:S(2)}) async-start(), calls=%async_computation.6 | async-start | bytes 4784128 | tf_op jit(solution)/shard_map/psum | solution.py:134
  11.1 388.2 %copy-start.34 = (f32[1,1024]{1,0:T(1,128)}, f32[1,1024]{1,0:T(1,128)S(1)}, u32[]{:S(2)}) copy-start(f32[1,1024]{1,0:T(1,128)S(1)} %get-tuple-element.253) | copy-start | bytes 12292
  12.6 386.6 %copy-start.30 = (f32[577]{0:T(1024)}, f32[577]{0:T(1024)S(1)}, u32[]{:S(2)}) copy-start(f32[577]{0:T(1024)S(1)} %broadcast_multiply_fusion.5) | copy-start | bytes 6928
  14.4 384.9 %copy-start.32 = (f32[577]{0:T(1024)}, f32[577]{0:T(1024)S(1)}, u32[]{:S(2)}) copy-start(f32[577]{0:T(1024)S(1)} %add_rsqrt_fusion.1) | copy-start | bytes 6928
  89.6 4.2 copy-start.8
  91.7 4.3 copy-start
  98.9 42.6 %copy-start.14 = (bf16[8,64,577]{2,1,0:T(8,128)(2,1)}, bf16[8,64,577]{2,1,0:T(8,128)(2,1)S(1)}, u32[]{:S(2)}) copy-start(bf16[8,64,577]{2,1,0:T(8,128)(2,1)S(1)} %fusion.115) | copy-start | bytes 1772548
  141.5 100.2 %all-gather.13.cloned.1.call-start = ((), (), s32[]{:S(2)}) async-start(), calls=%async_computation.7 | async-start | bytes 4456448 | tf_op jit(solution)/shard_map/all_gather | solution.py:173
  142.1 176.5 %all-gather.15.cloned.1.call-start = ((), (), s32[]{:S(2)}) async-start(), calls=%async_computation.8 | async-start | bytes 4456448 | tf_op jit(solution)/shard_map/all_gather | solution.py:174
  142.7 209.6 %all-reduce.10.cloned.1.call-start = ((), (), s32[]{:S(2)}) async-start(), calls=%async_computation.9 | async-start | bytes 4784128 | tf_op jit(solution)/shard_map/psum | solution.py:134
  164.7 242.1 %copy-start.2 = (f32[577,1024]{1,0:T(8,128)}, f32[577,1024]{1,0:T(8,128)S(1)}, u32[]{:S(2)}) copy-start(f32[577,1024]{1,0:T(8,128)S(1)} %get-tuple-element.237) | copy-start | bytes 7090180
  164.7 77.0 %copy-start.49 = (f32[2048]{0:T(1024)S(1)}, f32[2048]{0:T(1024)}, u32[]{:S(2)}) copy-start(f32[2048]{0:T(1024)} %param.36) | copy-start | bytes 24580
  318.6 9.0 copy-start.59
  331.7 112.4 %reduce-scatter.7.cloned.1.call-start = ((), (), s32[]{:S(2)}) async-start(), calls=%async_computation.11 | async-start | bytes 2228224 | tf_op jit(solution)/shard_map/reduce_scatter | solution.py:237
  361.3 218.5 %reduce-scatter.5.cloned.1.call-start = ((), (), s32[]{:S(2)}) async-start(), calls=%async_computation.10 | async-start | bytes 6684672 | tf_op jit(solution)/shard_map/reduce_scatter | solution.py:236
  389.5 3.4 copy-start.1
  398.2 8.5 copy-start.10
  406.7 355.2 %reduce-scatter.9.cloned.1.call-start = ((), (), s32[]{:S(2)}) async-start(), calls=%async_computation.12 | async-start | bytes 8912896 | tf_op jit(solution)/shard_map/reduce_scatter | solution.py:238
  414.5 530.4 %reduce-scatter.11.cloned.1.call-start = ((), (), s32[]{:S(2)}) async-start(), calls=%async_computation.13 | async-start | bytes 8912896 | tf_op jit(solution)/shard_map/reduce_scatter | solution.py:239
  423.1 21.0 %copy-start.29 = (f32[64,512]{1,0:T(8,128)S(1)}, f32[64,512]{1,0:T(8,128)}, u32[]{:S(2)}) copy-start(f32[64,512]{1,0:T(8,128)} %param.38) | copy-start | bytes 393220
  423.1 156.7 %copy-start.27 = (f32[64,3,512]{2,0,1:T(8,128)S(1)}, f32[64,3,512]{2,0,1:T(8,128)}, u32[]{:S(2)}) copy-start(f32[64,3,512]{2,0,1:T(8,128)} %param.37) | copy-start | bytes 1179652
  423.1 338.8 %copy-start.25 = (f32[64,2048]{1,0:T(8,128)S(1)}, f32[64,2048]{1,0:T(8,128)}, u32[]{:S(2)}) copy-start(f32[64,2048]{1,0:T(8,128)} %param.39) | copy-start | bytes 1572868
  423.1 521.8 %copy-start.26 = (f32[64,2048]{1,0:T(8,128)S(1)}, f32[64,2048]{1,0:T(8,128)}, u32[]{:S(2)}) copy-start(f32[64,2048]{1,0:T(8,128)} %param.40) | copy-start | bytes 1572868
  423.1 582.7 %all-gather.19.cloned.1.call-start = ((), (), s32[]{:S(2)}) async-start(), calls=%async_computation.15 | async-start | bytes 1114112 | tf_op jit(solution)/shard_map/all_gather | solution.py:263
  445.7 630.1 %all-gather.17.cloned.1.call-start = ((), (), s32[]{:S(2)}) async-start(), calls=%async_computation.14 | async-start | bytes 3342336 | tf_op jit(solution)/shard_map/all_gather | solution.py:263
  581.7 571.7 %all-gather.21.cloned.1.call-start = ((), (), s32[]{:S(2)}) async-start(), calls=%async_computation.16 | async-start | bytes 4456448 | tf_op jit(solution)/shard_map/all_gather | solution.py:263
  764.0 466.3 %all-gather.23.cloned.1.call-start = ((), (), s32[]{:S(2)}) async-start(), calls=%async_computation.17 | async-start | bytes 4456448 | tf_op jit(solution)/shard_map/all_gather | solution.py:263
  947.0 7.6 copy-start.22
  947.0 7.6 copy-start.23
  947.0 7.6 copy-start.24
  947.0 313.3 %all-reduce.12.cloned.1.call-start = ((), (), s32[]{:S(2)}) async-start(), calls=%async_computation.18 | async-start | bytes 9568256 | tf_op jit(solution)/shard_map/psum | solution.py:134
  947.5 7.1 copy-start.60
  958.1 1021.1 %all-reduce.14.cloned.1.call-start = ((), (), s32[]{:S(2)}) async-start(), calls=%async_computation.19 | async-start | bytes 25165824 | tf_op jit(solution)/shard_map/psum | solution.py:31
  1247.5 12.8 copy-start.31
  1247.6 12.8 copy-start.33
  1247.6 12.8 copy-start.35
  1247.6 15.9 copy-start.5
  1266.0 4.0 copy-start.45
  1266.0 4.0 copy-start.44
  1266.0 4.0 copy-start.56
  1266.0 444.9 %copy-start.43 = (f32[2,512]{1,0:T(2,128)S(1)}, f32[2,512]{1,0:T(2,128)}, u32[]{:S(2)}) copy-start(f32[2,512]{1,0:T(2,128)} %param.34) | copy-start | bytes 12292
  1266.0 444.9 %copy-start.57 = (f32[2,512]{1,0:T(2,128)S(1)}, f32[2,512]{1,0:T(2,128)}, u32[]{:S(2)}) copy-start(f32[2,512]{1,0:T(2,128)} %param.43) | copy-start | bytes 12292
  1266.1 445.5 %copy-start.36 = (f32[2,1024]{1,0:T(2,128)S(1)}, f32[2,1024]{1,0:T(2,128)}, u32[]{:S(2)}) copy-start(f32[2,1024]{1,0:T(2,128)} %param.32) | copy-start | bytes 24580
  1266.1 445.5 %copy-start.46 = (f32[2,1024]{1,0:T(2,128)S(1)}, f32[2,1024]{1,0:T(2,128)}, u32[]{:S(2)}) copy-start(f32[2,1024]{1,0:T(2,128)} %param.41) | copy-start | bytes 24580
  1266.1 446.1 %copy-start.37 = (f32[2,1024]{1,0:T(2,128)S(1)}, f32[2,1024]{1,0:T(2,128)}, u32[]{:S(2)}) copy-start(f32[2,1024]{1,0:T(2,128)} %param.33) | copy-start | bytes 24580
  1266.1 446.1 %copy-start.47 = (f32[2,1024]{1,0:T(2,128)S(1)}, f32[2,1024]{1,0:T(2,128)}, u32[]{:S(2)}) copy-start(f32[2,1024]{1,0:T(2,128)} %param.42) | copy-start | bytes 24580
  1266.1 446.7 %copy-start.39 = (f32[2,1024]{1,0:T(2,128)S(1)}, f32[2,1024]{1,0:T(2,128)}, u32[]{:S(2)}) copy-start(f32[2,1024]{1,0:T(2,128)} %param.35) | copy-start | bytes 24580
  1266.1 446.7 %copy-start.48 = (f32[2,1024]{1,0:T(2,128)S(1)}, f32[2,1024]{1,0:T(2,128)}, u32[]{:S(2)}) copy-start(f32[2,1024]{1,0:T(2,128)} %param.44) | copy-start | bytes 24580
  1266.1 447.3 %copy-start.50 = (f32[2048]{0:T(1024)S(1)}, f32[2048]{0:T(1024)}, u32[]{:S(2)}) copy-start(f32[2048]{0:T(1024)} %param.36) | copy-start | bytes 24580
  1266.1 447.3 %copy-start.51 = (f32[2048]{0:T(1024)S(1)}, f32[2048]{0:T(1024)}, u32[]{:S(2)}) copy-start(f32[2048]{0:T(1024)} %param.45) | copy-start | bytes 24580
  1266.2 447.9 %copy-start.3 = (f32[577,1024]{1,0:T(8,128)S(1)}, f32[577,1024]{1,0:T(8,128)}, u32[]{:S(2)}) copy-start(f32[577,1024]{1,0:T(8,128)} %copy-done.2) | copy-start | bytes 7090180
  1266.2 447.9 %copy-start.40 = (f32[1,1024]{1,0:T(1,128)S(1)}, f32[1,1024]{1,0:T(1,128)}, u32[]{:S(2)}) copy-start(f32[1,1024]{1,0:T(1,128)} %get-tuple-element.250) | copy-start | bytes 12292
  1710.9 6.5 copy-start.52
  1710.9 6.5 copy-start.53
  1710.9 6.5 copy-start.54
  1710.9 6.5 copy-start.55
  1710.9 6.5 copy-start.58
  1714.1 265.2 %copy-start.28 = (bf16[64,512]{1,0:T(8,128)(2,1)S(1)}, bf16[64,512]{1,0:T(8,128)(2,1)}, u32[]{:S(2)}) copy-start(bf16[64,512]{1,0:T(8,128)(2,1)} %param.29) | copy-start | bytes 196612
  1714.1 266.7 %copy-start.18 = (bf16[64,2048]{1,0:T(8,128)(2,1)S(1)}, bf16[64,2048]{1,0:T(8,128)(2,1)}, u32[]{:S(2)}) copy-start(bf16[64,2048]{1,0:T(8,128)(2,1)} %param.30) | copy-start | bytes 786436
  1714.1 268.5 %copy-start.19 = (bf16[64,2048]{1,0:T(8,128)(2,1)S(1)}, bf16[64,2048]{1,0:T(8,128)(2,1)}, u32[]{:S(2)}) copy-start(bf16[64,2048]{1,0:T(8,128)(2,1)} %param.31) | copy-start | bytes 786436
  1717.5 266.9 %copy-start.21 = (bf16[64,3,512]{2,0,1:T(8,128)(2,1)S(1)}, bf16[64,3,512]{2,0,1:T(8,128)(2,1)}, u32[]{:S(2)}) copy-start(bf16[64,3,512]{2,0,1:T(8,128)(2,1)} %param.28) | copy-start | bytes 589828
  (15 other events, 30.6 us)
Sparse Core Ops, SparseCore 0:
  10.8 70.5 all-gather.8
  84.2 53.7 all-gather.10
  141.6 20.6 all-reduce.7
  164.9 76.7 all-gather.12
  244.3 74.1 all-gather.14
  331.8 20.3 all-reduce.9
  361.4 82.6 reduce-scatter.6
  446.9 132.8 reduce-scatter.4
  582.7 179.1 reduce-scatter.8
  764.7 180.2 reduce-scatter.10
  948.3 57.5 all-gather.18
  1009.1 66.6 all-gather.16
  1079.2 74.2 all-gather.20
  1156.0 74.1 all-gather.22
  1232.7 27.6 all-reduce.11
  1266.6 712.5 all-reduce.13
where the time goes:
time: 2000 us; the launch traced here: 1990 us
  waiting for transfers between devices  1280 us (64%)
  blocking collectives  441 us (22%)
  matrix products  145 us (7%)
  other arithmetic  63 us (3%)
  local copies, waits for them, and re-layouts  39.1 us (2%)
    psum x1, blocking collectives, body(): lax.psum((gain_grad, nbias_grad, abias_grad, rbias_grad, ubias_grad), 'fs...  441 us
    psum x1, waiting for transfers between devices, spread(): return lax.psum(block, axis)  262 us
    all_gather x4, waiting for transfers between devices, body(): lax.all_gather(for_sending(shard_low), 'fsdp', axis=0, tiled=True)  198 us
    reduce_scatter x1, waiting for transfers between devices, body(): lax.psum_scatter(downw_grad, 'fsdp', scatter_dimension=0, tiled=True)  181 us
    reduce_scatter x1, waiting for transfers between devices, body(): lax.psum_scatter(upw_grad, 'fsdp', scatter_dimension=0, tiled=True)  180 us
    reduce_scatter x1, waiting for transfers between devices, body(): lax.psum_scatter(qkv_grad, 'fsdp', scatter_dimension=0, tiled=True)  134 us
    all_gather x1, waiting for transfers between devices, body(): lax.all_gather(up_weight, 'fsdp', axis=0, tiled=True)  76.6 us
    all_gather x1, waiting for transfers between devices, body(): lax.all_gather(down_weight, 'fsdp', axis=0, tiled=True)  69.2 us
  transfers between devices with their start and end apart: 16, of which 16 were waited for; matrix products, arithmetic and copies ran while one was open for 11% of the time, Pallas kernels for 0%

commit v1 on v0

--- a/solution.py
+++ b/solution.py
@@ -22,13 +22,220 @@
 ROOT_TWO_PI = 2.5066282746310002
 
 
-def for_sending(array):
-    return jax.tree.map(lambda a: a.astype(jnp.bfloat16) if a.dtype == jnp.float32 else a, array)
-
-
-def spread(block, axis, source):
-    block = jnp.where(lax.axis_index(axis) == source, block, jnp.zeros_like(block))
-    return lax.psum(block, axis)
+PLANE = 4
+
+
+def xor_pairs(count, bits):
+    return [(index, index ^ bits) for index in range(count)]
+
+
+def swap(block, bits):
+    return lax.ppermute(block, "fsdp", xor_pairs(lax.axis_size("fsdp"), bits))
+
+
+def place():
+    rank = lax.axis_index("fsdp")
+    return (rank % PLANE, rank // PLANE)
+
+
+def put(buffer, piece, index, axis):
+    return lax.dynamic_update_slice_in_dim(buffer, jnp.expand_dims(piece, axis), index, axis)
+
+
+def pick(buffer, index, axis):
+    return lax.dynamic_index_in_dim(buffer, index, axis, keepdims=False)
+
+
+def gather_rows(shard):
+    count = lax.axis_size("fsdp")
+    layers = count // PLANE
+    flat, layer = place()
+    rows, cols = shard.shape
+    half = cols // 2
+    column = jnp.zeros((layers, rows, cols), shard.dtype)
+    column = put(column, shard, layer, 0)
+    for step in range(1, layers):
+        column = put(column, swap(shard, PLANE * step), layer ^ step, 0)
+    from_x = swap(column, 1)
+    from_y = swap(column, 2)
+    across_x = swap(from_x[:, :, :half], 2)
+    across_y = swap(from_y[:, :, half:], 1)
+    whole = jnp.zeros((layers, PLANE, rows, cols), shard.dtype)
+    whole = put(whole, column, flat, 1)
+    whole = put(whole, from_x, flat ^ 1, 1)
+    whole = put(whole, from_y, flat ^ 2, 1)
+    whole = put(whole, jnp.concatenate([across_x, across_y], axis=2), flat ^ 3, 1)
+    return whole.reshape(count * rows, cols)
+
+
+def wide(block):
+    return block.astype(jnp.float32)
+
+
+def scatter_sum(partial_sum):
+    count = lax.axis_size("fsdp")
+    layers = count // PLANE
+    flat, layer = place()
+    cols = partial_sum.shape[1]
+    rows = partial_sum.shape[0] // count
+    half = cols // 2
+    low = partial_sum.astype(jnp.bfloat16).reshape(layers, PLANE, rows, cols)
+    mine = pick(low, flat, 1)
+    to_x = pick(low, flat ^ 1, 1)
+    to_y = pick(low, flat ^ 2, 1)
+    to_far = pick(low, flat ^ 3, 1)
+    left = swap(to_far[:, :, :half], 1)
+    right = swap(to_far[:, :, half:], 2)
+    to_y = jnp.concatenate(
+        [(wide(to_y[:, :, :half]) + wide(left)).astype(jnp.bfloat16), to_y[:, :, half:]], axis=2
+    )
+    to_x = jnp.concatenate(
+        [to_x[:, :, :half], (wide(to_x[:, :, half:]) + wide(right)).astype(jnp.bfloat16)], axis=2
+    )
+    total = wide(mine) + wide(swap(to_x, 1)) + wide(swap(to_y, 2))
+    total_low = total.astype(jnp.bfloat16)
+    result = pick(total, layer, 0)
+    for step in range(1, layers):
+        result = result + wide(swap(pick(total_low, layer ^ step, 0), PLANE * step))
+    return result
+
+
+def total_everywhere(vector):
+    bits = 1
+    while bits < lax.axis_size("fsdp"):
+        vector = vector + swap(vector, bits)
+        bits *= 2
+    return vector
+
+
+def send(block, pairs):
+    return lax.ppermute(block, ("fsdp", "tensor"), sorted(pairs))
+
+
+def wide_owners(layers):
+    return {
+        (0, 0): PLANE * (1 % layers),
+        (0, 1): PLANE * (2 % layers) + 1,
+        (1, 0): PLANE * (2 % layers) + 3,
+        (1, 1): PLANE * (1 % layers) + 2,
+    }
+
+
+def holds_up(flat, half):
+    return (flat & 1) == half
+
+
+def bring_wide(up_rows, down_rows):
+    layers = lax.axis_size("fsdp") // PLANE
+    owners = wide_owners(layers)
+    flat, _ = place()
+    keep_up = holds_up(flat, lax.axis_index("tensor"))
+    kept = jnp.where(keep_up, up_rows, down_rows)
+    sent = jnp.where(keep_up, down_rows, up_rows)
+    kept = jnp.concatenate([kept, swap(sent, 1)], axis=0)
+    pairs = []
+    for (_, half), owner in owners.items():
+        for layer in range(layers):
+            target = PLANE * layer + owner % PLANE
+            pairs.append(((target ^ 2) * 2 + half, target * 2 + half))
+    kept = jnp.concatenate([kept, send(kept, pairs)], axis=0)
+    pieces = [kept]
+    for step in range(1, layers):
+        pairs = [((o ^ (PLANE * step)) * 2 + half, o * 2 + half) for (_, half), o in owners.items()]
+        pieces.append(send(kept, pairs))
+    return jnp.concatenate(pieces, axis=0)
+
+
+def return_wide(matrix):
+    layers = lax.axis_size("fsdp") // PLANE
+    owners = wide_owners(layers)
+    flat, layer = place()
+    half = lax.axis_index("tensor")
+    plane_rows = matrix.shape[0] // layers
+    rows = plane_rows // PLANE
+    is_owner = owner_here()
+    mine = jnp.where(is_owner, matrix[:plane_rows], jnp.zeros_like(matrix[:plane_rows]))
+    for step in range(1, layers):
+        pairs = [(o * 2 + side, (o ^ (PLANE * step)) * 2 + side) for (_, side), o in owners.items()]
+        mine = mine + send(matrix[plane_rows * step : plane_rows * (step + 1)], pairs)
+    blocks = [mine[rows * index : rows * (index + 1)] for index in range(PLANE)]
+    found = [blocks[0]]
+    for bits in range(1, PLANE):
+        pairs = []
+        for (_, side), owner in owners.items():
+            for level in range(layers):
+                source = PLANE * level + owner % PLANE
+                pairs.append((source * 2 + side, (source ^ bits) * 2 + side))
+        found.append(send(blocks[bits], pairs))
+    found = jnp.stack(found)
+    up_at = jnp.where(half == 0, owners[0, 0] % PLANE, owners[0, 1] % PLANE)
+    down_at = jnp.where(half == 0, owners[1, 0] % PLANE, owners[1, 1] % PLANE)
+    return (pick(found, flat ^ up_at, 0), pick(found, flat ^ down_at, 0))
+
+
+def owner_here():
+    owners = wide_owners(lax.axis_size("fsdp") // PLANE)
+    rank = lax.axis_index("fsdp")
+    half = lax.axis_index("tensor")
+    answer = False
+    for (_, side), owner in owners.items():
+        answer = answer | ((rank == owner) & (half == side))
+    return answer
+
+
+def bring_narrow(blocks):
+    layers = lax.axis_size("fsdp") // PLANE
+    flat, _ = place()
+    odd_x = (flat & 1) == 1
+    odd_y = (flat & 2) == 2
+    even = jnp.concatenate([blocks[0], blocks[2]], axis=0)
+    odd = jnp.concatenate([blocks[1], blocks[3]], axis=0)
+    kept = jnp.where(odd_x, odd, even)
+    got = swap(jnp.where(odd_x, even, odd), 1)
+    rows = blocks[0].shape[0]
+    low_part = jnp.concatenate([kept[:rows], got[:rows]], axis=0)
+    high_part = jnp.concatenate([kept[rows:], got[rows:]], axis=0)
+    kept = jnp.where(odd_y, high_part, low_part)
+    got = swap(jnp.where(odd_y, low_part, high_part), 2)
+    kept = jnp.concatenate([kept, got], axis=0)
+    return jnp.concatenate(
+        [kept] + [swap(kept, PLANE * step) for step in range(1, layers)], axis=0
+    )
+
+
+def return_narrow(mine):
+    flat, _ = place()
+    rows = mine.shape[0] // PLANE
+    blocks = [mine[rows * index : rows * (index + 1)] for index in range(PLANE)]
+    found = jnp.stack([blocks[0]] + [swap(blocks[bits], bits) for bits in range(1, PLANE)])
+    return [pick(found, flat ^ index, 0) for index in range(PLANE)]
+
+
+def low_dot(left, right, dims):
+    return lax.dot_general(
+        left.astype(jnp.bfloat16),
+        right.astype(jnp.bfloat16),
+        (dims, ((), ())),
+        preferred_element_type=jnp.float32,
+    )
+
+
+def orthogonal(matrix):
+    count = matrix.shape[0]
+    current = matrix.astype(jnp.float32)
+    norm_value = jnp.sqrt(jnp.sum(current * current))
+    current = current / (norm_value + NS_EPS)
+    row = lax.broadcasted_iota(jnp.int32, (count, count), 0)
+    on_diagonal = row == lax.broadcasted_iota(jnp.int32, (count, count), 1)
+    for repeat in range(NS_STEPS):
+        gram = low_dot(current, current, ((1,), (1,)))
+        level = jnp.sum(current * current) / count
+        rest = jnp.where(on_diagonal, gram - level, gram)
+        square = low_dot(rest, rest, ((1,), (0,)))
+        poly = (COEF_B + 2.0 * COEF_C * level) * rest + COEF_C * square
+        keep = COEF_A + COEF_B * level + COEF_C * level * level
+        current = keep * current + low_dot(poly, current, ((1,), (0,)))
+    return current.astype(jnp.bfloat16)
 
 
 def gelu_value(upper):
@@ -55,26 +262,6 @@
         - jnp.mean(scaled, axis=-1, keepdims=True)
         - normed * jnp.mean(scaled * normed, axis=-1, keepdims=True)
     )
-
-
-def orthogonal(matrix):
-    rows, cols = matrix.shape
-    current = matrix.astype(jnp.float32)
-    if rows > cols:
-        current = current.T
-    norm_value = jnp.sqrt(jnp.sum(current * current))
-    current = current / (norm_value + NS_EPS)
-    for repeat in range(NS_STEPS):
-        gram = jnp.dot(current, current.T, precision=HIGHEST)
-        poly = COEF_B * gram + COEF_C * jnp.dot(gram, gram, precision=HIGHEST)
-        current = COEF_A * current + jnp.dot(poly, current, precision=HIGHEST)
-    if rows > cols:
-        current = current.T
-    return current
-
-
-def zero_float(matrix):
-    return jnp.zeros(matrix.shape, jnp.float32)
 
 
 def split_heads(block):
@@ -131,14 +318,7 @@
 
 
 def tensor_total(partial_sum):
-    return lax.psum(partial_sum, "tensor")
-
-
-def pick_owned(matrices, marks, rank):
-    chosen = jnp.zeros_like(matrices[0])
-    for matrix, mark in zip(matrices, marks):
-        chosen = jnp.where(rank == mark, matrix, chosen)
-    return chosen
+    return partial_sum + lax.ppermute(partial_sum, "tensor", [(0, 1), (1, 0)])
 
 
 def body(
@@ -163,18 +343,15 @@
     rbias_moment,
     ubias_moment,
 ):
-    rank = lax.axis_index("fsdp")
-    fsdp_count = lax.axis_size("fsdp")
-    owner_list = [index * fsdp_count // 6 for index in range(6)]
     shard_rows = qkv_weight.shape[0]
-    qkv_full, out_full, up_full, down_full = (
-        lax.all_gather(qkv_weight, "fsdp", axis=0, tiled=True),
-        lax.all_gather(out_weight, "fsdp", axis=0, tiled=True),
-        lax.all_gather(up_weight, "fsdp", axis=0, tiled=True),
-        lax.all_gather(down_weight, "fsdp", axis=0, tiled=True),
-    )
+    head_width = qkv_weight.shape[2]
+    first = jnp.concatenate([qkv_weight.reshape(shard_rows, -1), out_weight], axis=1)
+    first = gather_rows(first)
+    qkv_full = first[:, : 3 * head_width].reshape(-1, 3, head_width)
+    out_full = first[:, 3 * head_width :]
+    up_full = gather_rows(up_weight)
+    down_full = gather_rows(down_weight)
     image_count, length, width = images.shape
-    head_width = qkv_full.shape[2]
     tokens = images.reshape(-1, width).astype(jnp.float32)
     hat_one, inv_one = layer_stats(tokens)
     normed1 = (hat_one * norm_gain[0] + norm_bias[0]).astype(jnp.bfloat16)
@@ -182,7 +359,8 @@
     bias_three = jnp.stack([attn_bias[0], jnp.zeros_like(attn_bias[0]), attn_bias[1]])
     proj = (proj + bias_three).astype(jnp.bfloat16)
     proj_images = proj.reshape(image_count, length, 3, head_width)
-    attn_images, log_totals = lax.map(attend, proj_images)
+    attended = [attend(proj_images[index]) for index in range(image_count)]
+    attn_images = jnp.stack([item[0] for item in attended])
     attn_rows = attn_images.reshape(-1, head_width)
     branch = tensor_total(
         jnp.einsum("th,dh->td", attn_rows, out_full, preferred_element_type=jnp.float32)
@@ -213,8 +391,12 @@
     mid_low = mid_grad.astype(jnp.bfloat16)
     outw_grad = jnp.einsum("td,th->dh", mid_low, attn_rows, preferred_element_type=jnp.float32)
     attn_grad = jnp.dot(mid_low, out_full, preferred_element_type=jnp.float32).astype(jnp.bfloat16)
-    proj_grad = lax.map(
-        attend_back, (proj_images, log_totals, attn_grad.reshape(image_count, length, head_width))
+    mixed_grads = attn_grad.reshape(image_count, length, head_width)
+    proj_grad = jnp.stack(
+        [
+            attend_back((proj_images[index], attended[index][1], mixed_grads[index]))
+            for index in range(image_count)
+        ]
     )
     proj_grad = proj_grad.reshape(-1, 3, head_width)
     qkv_grad = jnp.einsum("td,tjh->djh", normed1, proj_grad, preferred_element_type=jnp.float32)
@@ -232,13 +414,26 @@
     input_grad = mid_grad + norm_back(normed1_grad, hat_one, inv_one, norm_gain[0])
     gain_grad = jnp.stack([gain_one, gain_two])
     nbias_grad = jnp.stack([shift_one, shift_two])
+    down_shard = scatter_sum(downw_grad)
+    up_shard = scatter_sum(upw_grad)
+    first_shard = scatter_sum(
+        jnp.concatenate([qkv_grad.reshape(width, -1), outw_grad], axis=1)
+    )
     grad_shards = (
-        lax.psum_scatter(qkv_grad, "fsdp", scatter_dimension=0, tiled=True),
-        lax.psum_scatter(outw_grad, "fsdp", scatter_dimension=0, tiled=True),
-        lax.psum_scatter(upw_grad, "fsdp", scatter_dimension=0, tiled=True),
-        lax.psum_scatter(downw_grad, "fsdp", scatter_dimension=0, tiled=True),
-    )
-    vector_grads = lax.psum((gain_grad, nbias_grad, abias_grad, rbias_grad, ubias_grad), "fsdp")
+        first_shard[:, : 3 * head_width].reshape(shard_rows, 3, head_width),
+        first_shard[:, 3 * head_width :],
+        up_shard,
+        down_shard,
+    )
+    vector_list = (gain_grad, nbias_grad, abias_grad, rbias_grad, ubias_grad)
+    packed = jnp.concatenate([item.reshape(-1, 128) for item in vector_list], axis=0)
+    packed = total_everywhere(packed)
+    vector_grads = []
+    start = 0
+    for item in vector_list:
+        lines = item.size // 128
+        vector_grads.append(packed[start : start + lines].reshape(item.shape))
+        start += lines
     moment_shards = tuple(
         (
             MOMENTUM * stored + gradient
@@ -256,32 +451,19 @@
         up_weight,
         down_weight,
     ]
-    owns_narrow = jnp.any(jnp.array(owner_list[:4], jnp.int32) == rank)
-    owns_wide = jnp.any(jnp.array(owner_list[4:], jnp.int32) == rank)
-    low_moments = jax.tree.map(
-        lambda part, own: part.astype(own.dtype),
-        lax.all_gather(for_sending(shard_low), "fsdp", axis=0, tiled=True),
-        shard_low,
-    )
-    matrices = [
-        low_moments[0][:, 0],
-        low_moments[0][:, 1],
-        low_moments[0][:, 2],
-        low_moments[1],
-        low_moments[2],
-        low_moments[3],
-    ]
-    narrow_pick = pick_owned(matrices[:4], owner_list[:4], rank)
-    wide_pick = pick_owned(matrices[4:], owner_list[4:], rank)
-    narrow_orth = lax.cond(owns_narrow, orthogonal, zero_float, narrow_pick)
-    wide_orth = lax.cond(owns_wide, orthogonal, zero_float, wide_pick)
+    wide_block = bring_wide(shard_low[2], shard_low[3])
+    wide_orth = lax.cond(owner_here(), orthogonal, jnp.zeros_like, wide_block)
+    up_orth, down_orth = return_wide(wide_orth)
+    narrow_block = bring_narrow(
+        [shard_low[0][:, 0], shard_low[0][:, 1], shard_low[0][:, 2], shard_low[1]]
+    )
+    plane_rows = PLANE * shard_rows
+    narrow_orth = orthogonal(narrow_block.T).T[:plane_rows]
+    pieces = return_narrow(narrow_orth) + [up_orth, down_orth]
     updated = []
-    for index in range(6):
-        chosen = narrow_orth if index < 4 else wide_orth
-        chosen = spread(chosen.astype(jnp.bfloat16), "fsdp", owner_list[index]).astype(chosen.dtype)
-        piece = lax.dynamic_slice_in_dim(chosen, rank * shard_rows, shard_rows, 0)
-        factor = 0.2 * math.sqrt(max(chosen.shape[0], chosen.shape[1]))
-        updated.append(weight_shards[index].astype(jnp.float32) - MUON_RATE * (piece * factor))
+    for stored, piece in zip(weight_shards, pieces):
+        factor = 0.2 * math.sqrt(max(width, piece.shape[1]))
+        updated.append(stored.astype(jnp.float32) - MUON_RATE * (piece.astype(jnp.float32) * factor))
     qkv_new = jnp.stack(updated[:3], axis=1)
     out_new = updated[3]
     up_new = updated[4]

time: 2000 us -> 803 us (0.40)
  the two profiles are of different devices: /device:TPU:0 before, /device:TPU:16 now
where the time goes in v1:
time: 803 us; the launch traced here: 791 us
  starting transfers between devices  236 us (29%)
  waiting for transfers between devices  230 us (29%)
  matrix products  121 us (15%)
  local copies, waits for them, and re-layouts  105 us (13%)
  other arithmetic  75.3 us (9%)
  between operations  19.9 us (2%)
    ppermute x55, starting transfers between devices, swap(): return lax.ppermute(block, 'fsdp', xor_pairs(lax.axis_size('fsdp'), bits))  220 us
    ppermute x55, waiting for transfers between devices, swap(): return lax.ppermute(block, 'fsdp', xor_pairs(lax.axis_size('fsdp'), bits))  210 us
    dot_general x10, matrix products, low_dot(): lax.dot_general(left.astype(jnp.bfloat16), right.astype(jnp.bfloat16), (d...  40.3 us
    unnamed x215, local copies, waits for them, and re-layouts  34.1 us
    ppermute x10, waiting for transfers between devices, send(): return lax.ppermute(block, ('fsdp', 'tensor'), sorted(pairs))  20.7 us
  transfers between devices with their start and end apart: 69, of which 29 were waited for; matrix products, arithmetic and copies ran while one was open for 33% of the time, Pallas kernels for 0%

profile of v1, /device:TPU:16, one launch (start us, length us, event | category | flops | bytes accessed | tf_op | source)
XLA Modules:
  0.0 790.6 jit_solution(17025526499706207184)
XLA Ops:
  24.1 3.1 collective-permute-done
  31.7 8.1 %collective-permute-done.10 = bf16[64,2048]{1,0:T(8,128)(2,1)} collective-permute-done((bf16[64,2048]{1,0:T(8,128)(2,1)}, bf16[64,2048]{1,0:T(8,128)(2,1)}, u32[]{:S(2)}, u32[]{:S(2)}) %collective-permute-start.10) | collective-permute-done | bytes 262176 | tf_op jit(solution)/shard_map/ppermute | solution.py:33
  41.3 13.4 %collective-permute-done.1 = bf16[64,2048]{1,0:T(8,128)(2,1)} collective-permute-done((bf16[64,2048]{1,0:T(8,128)(2,1)}, bf16[64,2048]{1,0:T(8,128)(2,1)}, u32[]{:S(2)}, u32[]{:S(2)}) %collective-permute-start.1) | collective-permute-done | bytes 262176 | tf_op jit(solution)/shard_map/ppermute | solution.py:33
  57.8 4.4 collective-permute-done.2
  68.0 4.1 collective-permute-done.17
  75.0 22.1 %collective-permute-done.3 = bf16[4,64,2048]{2,1,0:T(8,128)(2,1)S(1)} collective-permute-done((bf16[4,64,2048]{2,1,0:T(8,128)(2,1)}, bf16[4,64,2048]{2,1,0:T(8,128)(2,1)S(1)}, u32[]{:S(2)}, u32[]{:S(2)}) %collective-permute-start.3) | collective-permute-done | bytes 1048608 | tf_op jit(solution)/shard_map/ppermute | solution.py:33
  102.1 8.6 %collective-permute-done.4 = bf16[4,64,2048]{2,1,0:T(8,128)(2,1)S(1)} collective-permute-done((bf16[4,64,2048]{2,1,0:T(8,128)(2,1)}, bf16[4,64,2048]{2,1,0:T(8,128)(2,1)S(1)}, u32[]{:S(2)}, u32[]{:S(2)}) %collective-permute-start.4) | collective-permute-done | bytes 1048608 | tf_op jit(solution)/shard_map/ppermute | solution.py:33
  116.3 3.3 collective-permute-done.18
  121.8 11.4 %collective-permute-done.19 = bf16[4,64,2048]{2,1,0:T(8,128)(2,1)S(1)} collective-permute-done((bf16[4,64,2048]{2,1,0:T(8,128)(2,1)}, bf16[4,64,2048]{2,1,0:T(8,128)(2,1)S(1)}, u32[]{:S(2)}, u32[]{:S(2)}) %collective-permute-start.19) | collective-permute-done | bytes 1048608 | tf_op jit(solution)/shard_map/ppermute | solution.py:33
  135.7 8.7 %collective-permute-done.5 = bf16[4,64,1024]{2,1,0:T(8,128)(2,1)S(1)} collective-permute-done((bf16[4,64,1024]{2,1,0:T(8,128)(2,1)S(1)}, bf16[4,64,1024]{2,1,0:T(8,128)(2,1)S(1)}, u32[]{:S(2)}, u32[]{:S(2)}) %collective-permute-start.5) | collective-permute-done | bytes 524320 | tf_op jit(solution)/shard_map/ppermute | solution.py:33
  150.0 4.6 copy.82
  154.6 5.5 add_convert_fusion.6
  160.1 2.7 copy.84
  169.3 3.1 fusion.84
  181.6 3.4 multiply_convert_fusion.1
  185.0 4.7 convert_reduce_fusion
  189.7 4.1 fusion.224
  193.8 4.5 convolution_convert_fusion.2
  203.6 4.1 fusion.223
  212.9 2.8 collective-permute-done.32
  218.6 6.4 collective-permute-done.34
  226.8 3.6 multiply_reduce_fusion.7
  230.5 4.1 fusion.194
  236.0 2.8 convolution_convert_fusion.4
  241.0 11.8 %multiply_reduce_fusion.5 = (f32[8,577]{1,0:T(8,128)S(1)}, f32[8,577,577]{1,2,0:T(8,128)}) fusion(f32[8,577,577]{1,2,0:T(8,128)} %copy-done, f32[8,577]{1,0:T(8,128)S(1)} %log_add_fusion, bf16[577,8,64]{0,2,1:T(8,128)(2,1)} %bitcast.382, bf16[577,3,8,64]{0,3,2,1:T(8,128)(2,1)S(1)} %bitcast.376), kind=kOutput, calls=%fused_computation.49 | convolution fusion | flops 351568384 | bytes 22592608 | tf_op jit(solution)/shard_map/qhe,khe->hqk/dot_general | solution.py:300
  252.8 7.5 fusion.81
  260.4 6.4 multiply_convert_fusion
  268.9 2.7 fusion.80
  275.6 5.6 convolution_bitcast_fusion
  281.3 5.1 convolution_convert_fusion.1
  286.4 3.8 fusion.197
  295.5 6.3 convolution_convert_fusion
  301.8 4.7 fusion.57
  307.2 5.4 convert_bitcast_fusion.1
  314.4 2.6 convolution_convert_fusion.3
  332.7 3.8 copy.118
  346.5 4.7 collective-permute-done.25
  357.0 17.5 %collective-permute-done.40 = bf16[4,64,2048]{2,1,0:T(8,128)(2,1)S(1)} collective-permute-done((bf16[4,64,2048]{2,1,0:T(8,128)(2,1)S(1)}, bf16[4,64,2048]{2,1,0:T(8,128)(2,1)S(1)}, u32[]{:S(2)}, u32[]{:S(2)}) %collective-permute-start.40) | collective-permute-done | bytes 1048608 | tf_op jit(solution)/shard_map/ppermute | solution.py:33
  377.2 3.1 fusion.195
  381.2 14.3 %collective-permute-done.26 = bf16[4,64,2048]{2,1,0:T(8,128)(2,1)S(1)} collective-permute-done((bf16[4,64,2048]{2,1,0:T(8,128)(2,1)S(1)}, bf16[4,64,2048]{2,1,0:T(8,128)(2,1)S(1)}, u32[]{:S(2)}, u32[]{:S(2)}) %collective-permute-start.26) | collective-permute-done | bytes 1048608 | tf_op jit(solution)/shard_map/ppermute | solution.py:33
  409.0 4.2 collective-permute-done.44
  413.2 10.0 %collective-permute-done.45 = bf16[64,2048]{1,0:T(8,128)(2,1)S(1)} collective-permute-done((bf16[64,2048]{1,0:T(8,128)(2,1)}, bf16[64,2048]{1,0:T(8,128)(2,1)S(1)}, u32[]{:S(2)}, u32[]{:S(2)}) %collective-permute-start.45) | collective-permute-done | bytes 262176 | tf_op jit(solution)/shard_map/ppermute | solution.py:33
  423.9 3.0 broadcast_select_fusion
  428.1 25.7 %collective-permute-done.30 = bf16[64,2048]{0,1:T(8,128)(2,1)S(1)} collective-permute-done((bf16[64,2048]{0,1:T(8,128)(2,1)}, bf16[64,2048]{0,1:T(8,128)(2,1)S(1)}, u32[]{:S(2)}, u32[]{:S(2)}) %collective-permute-start.30) | collective-permute-done | bytes 262176 | tf_op jit(solution)/shard_map/ppermute | solution.py:33
  453.8 11.8 %collective-permute-done.31 = bf16[64,2048]{0,1:T(8,128)(2,1)S(1)} collective-permute-done((bf16[64,2048]{0,1:T(8,128)(2,1)}, bf16[64,2048]{0,1:T(8,128)(2,1)S(1)}, u32[]{:S(2)}, u32[]{:S(2)}) %collective-permute-start.31) | collective-permute-done | bytes 262176 | tf_op jit(solution)/shard_map/ppermute | solution.py:33
  469.3 4.1 collective-permute-done.50
  475.5 3.1 collective-permute-done.51
  485.3 2.6 collective-permute-done.52
  488.0 8.1 %collective-permute-done.53 = bf16[256,512]{0,1:T(8,128)(2,1)S(1)} collective-permute-done((bf16[256,512]{0,1:T(8,128)(2,1)S(1)}, bf16[256,512]{0,1:T(8,128)(2,1)S(1)}, u32[]{:S(2)}, u32[]{:S(2)}) %collective-permute-start.53) | collective-permute-done | bytes 262176 | tf_op jit(solution)/shard_map/ppermute | solution.py:33
  496.1 5.6 collective-permute-done.54
  509.7 4.0 multiply_reduce_fusion.15
  518.7 6.3 multiply_reduce_fusion.14
  530.0 6.4 multiply_reduce_fusion.13
  541.4 5.0 multiply_reduce_fusion.12
  549.6 4.0 fusion.177
  561.3 7.6 fusion.70
  575.4 7.9 %collective-permute-done.62 = bf16[256,2048]{1,0:T(8,128)(2,1)} collective-permute-done((bf16[256,2048]{1,0:T(8,128)(2,1)}, bf16[256,2048]{1,0:T(8,128)(2,1)}, u32[]{:S(2)}, u32[]{:S(2)}) %collective-permute-start.62) | collective-permute-done | bytes 1048608 | tf_op jit(solution)/shard_map/ppermute | solution.py:112
  585.7 5.6 conditional.1
  585.7 2.6 broadcast.177
  591.4 3.7 fusion.203
  600.6 155.2 %collective-permute-start.56 = (bf16[64,512]{0,1:T(8,128)(2,1)}, bf16[64,512]{0,1:T(8,128)(2,1)}, u32[]{:S(2)}, u32[]{:S(2)}) collective-permute-start(bf16[64,512]{0,1:T(8,128)(2,1)} %get-tuple-element.171), channel_id=1, source_target_pairs={{0,4},{2,6},{4,0},{6,2},{8,12},{10,14},{12,8},{14,10},{16,20},{18,... | collective-permute-start | bytes 196616 | tf_op jit(solution)/shard_map/ppermute | solution.py:33
  755.7 4.3 collective-permute-start.57
  766.3 7.6 collective-permute-done.65
  784.1 3.8 collective-permute-done.68
  (484 shorter events, 221.7 us)
Async XLA Ops:
  0.7 20.9 %collective-permute-start.8 = (bf16[64,2048]{1,0:T(8,128)(2,1)}, bf16[64,2048]{1,0:T(8,128)(2,1)}, u32[]{:S(2)}, u32[]{:S(2)}) collective-permute-start(bf16[64,2048]{1,0:T(8,128)(2,1)} %param.26), channel_id=1, source_target_pairs={{0,8},{2,10},{4,12},{6,14},{8,0},{10,2},{12,4},{14,6},{16,24},{18,... | collective-permute-start | bytes 786440 | tf_op jit(solution)/shard_map/ppermute | solution.py:33
  2.3 26.9 %collective-permute-start.9 = (bf16[64,2048]{1,0:T(8,128)(2,1)}, bf16[64,2048]{1,0:T(8,128)(2,1)}, u32[]{:S(2)}, u32[]{:S(2)}) collective-permute-start(bf16[64,2048]{1,0:T(8,128)(2,1)} %param.26), channel_id=1, source_target_pairs={{0,16},{2,18},{4,20},{6,22},{8,24},{10,26},{12,28},{14,30},{16,0},... | collective-permute-start | bytes 786440 | tf_op jit(solution)/shard_map/ppermute | solution.py:33
  2.7 37.2 %collective-permute-start.10 = (bf16[64,2048]{1,0:T(8,128)(2,1)}, bf16[64,2048]{1,0:T(8,128)(2,1)}, u32[]{:S(2)}, u32[]{:S(2)}) collective-permute-start(bf16[64,2048]{1,0:T(8,128)(2,1)} %param.26), channel_id=1, source_target_pairs={{0,24},{2,26},{4,28},{6,30},{8,16},{10,18},{12,20},{14,22},{16,8},... | collective-permute-start | bytes 786440 | tf_op jit(solution)/shard_map/ppermute | solution.py:33
  7.3 19.8 %collective-permute-start = (bf16[64,2048]{1,0:T(8,128)(2,1)}, bf16[64,2048]{1,0:T(8,128)(2,1)}, u32[]{:S(2)}, u32[]{:S(2)}) collective-permute-start(bf16[64,2048]{1,0:T(8,128)(2,1)} %constant_dynamic-update-slice_fusion), channel_id=1, source_target_pairs={{0,8},{2,10},{4,12},{6,14},{8,0},{10,2},{12,4},{14,6},{16,24},{18,... | collective-permute-start | bytes 786440 | tf_op jit(solution)/shard_map/ppermute | solution.py:33
  9.8 44.9 %collective-permute-start.1 = (bf16[64,2048]{1,0:T(8,128)(2,1)}, bf16[64,2048]{1,0:T(8,128)(2,1)}, u32[]{:S(2)}, u32[]{:S(2)}) collective-permute-start(bf16[64,2048]{1,0:T(8,128)(2,1)} %constant_dynamic-update-slice_fusion), channel_id=1, source_target_pairs={{0,16},{2,18},{4,20},{6,22},{8,24},{10,26},{12,28},{14,30},{16,0},... | collective-permute-start | bytes 786440 | tf_op jit(solution)/shard_map/ppermute | solution.py:33
  21.6 40.7 %collective-permute-start.2 = (bf16[64,2048]{1,0:T(8,128)(2,1)}, bf16[64,2048]{1,0:T(8,128)(2,1)S(1)}, u32[]{:S(2)}, u32[]{:S(2)}) collective-permute-start(bf16[64,2048]{1,0:T(8,128)(2,1)} %constant_dynamic-update-slice_fusion), channel_id=1, source_target_pairs={{0,24},{2,26},{4,28},{6,30},{8,16},{10,18},{12,20},{14,22},{16,8},... | collective-permute-start | bytes 786440 | tf_op jit(solution)/shard_map/ppermute | solution.py:33
  27.2 37.3 %collective-permute-start.15 = (bf16[64,2048]{1,0:T(8,128)(2,1)}, bf16[64,2048]{1,0:T(8,128)(2,1)S(1)}, u32[]{:S(2)}, u32[]{:S(2)}) collective-permute-start(bf16[64,2048]{1,0:T(8,128)(2,1)} %param.27), channel_id=1, source_target_pairs={{0,8},{2,10},{4,12},{6,14},{8,0},{10,2},{12,4},{14,6},{16,24},{18,... | collective-permute-start | bytes 786440 | tf_op jit(solution)/shard_map/ppermute | solution.py:33
  29.2 37.5 %collective-permute-start.16 = (bf16[64,2048]{1,0:T(8,128)(2,1)S(1)}, bf16[64,2048]{1,0:T(8,128)(2,1)S(1)}, u32[]{:S(2)}, u32[]{:S(2)}) collective-permute-start(bf16[64,2048]{1,0:T(8,128)(2,1)S(1)} %copy-done.59), channel_id=1, source_target_pairs={{0,16},{2,18},{4,20},{6,22},{8,24},{10,26},{12,28},{14,30},{16,0},... | collective-permute-start | bytes 786440 | tf_op jit(solution)/shard_map/ppermute | solution.py:33
  39.9 32.2 %collective-permute-start.17 = (bf16[64,2048]{1,0:T(8,128)(2,1)S(1)}, bf16[64,2048]{1,0:T(8,128)(2,1)S(1)}, u32[]{:S(2)}, u32[]{:S(2)}) collective-permute-start(bf16[64,2048]{1,0:T(8,128)(2,1)S(1)} %copy-done.59), channel_id=1, source_target_pairs={{0,24},{2,26},{4,28},{6,30},{8,16},{10,18},{12,20},{14,22},{16,8},... | collective-permute-start | bytes 786440 | tf_op jit(solution)/shard_map/ppermute | solution.py:33
  54.7 57.6 %collective-permute-start.11 = (bf16[4,64,2048]{2,1,0:T(8,128)(2,1)S(1)}, bf16[4,64,2048]{2,1,0:T(8,128)(2,1)S(1)}, u32[]{:S(2)}, u32[]{:S(2)}) collective-permute-start(bf16[4,64,2048]{2,1,0:T(8,128)(2,1)S(1)} %bitcast_dynamic-update-slice_fusion.13), channel_id=1, source_target_pairs={{0,2},{2,0},{4,6},{6,4},{8,10},{10,8},{12,14},{14,12},{16,18},{18,... | collective-permute-start | bytes 3145736 | tf_op jit(solution)/shard_map/ppermute | solution.py:33
  62.2 52.6 %collective-permute-start.12 = (bf16[4,64,2048]{2,1,0:T(8,128)(2,1)S(1)}, bf16[4,64,2048]{2,1,0:T(8,128)(2,1)S(1)}, u32[]{:S(2)}, u32[]{:S(2)}) collective-permute-start(bf16[4,64,2048]{2,1,0:T(8,128)(2,1)S(1)} %bitcast_dynamic-update-slice_fusion.13), channel_id=1, source_target_pairs={{0,4},{2,6},{4,0},{6,2},{8,12},{10,14},{12,8},{14,10},{16,20},{18,... | collective-permute-start | bytes 3145736 | tf_op jit(solution)/shard_map/ppermute | solution.py:33
  64.5 32.6 %collective-permute-start.3 = (bf16[4,64,2048]{2,1,0:T(8,128)(2,1)}, bf16[4,64,2048]{2,1,0:T(8,128)(2,1)S(1)}, u32[]{:S(2)}, u32[]{:S(2)}) collective-permute-start(bf16[4,64,2048]{2,1,0:T(8,128)(2,1)} %bitcast_dynamic-update-slice_fusion.17), channel_id=1, source_target_pairs={{0,2},{2,0},{4,6},{6,4},{8,10},{10,8},{12,14},{14,12},{16,18},{18,... | collective-permute-start | bytes 3145736 | tf_op jit(solution)/shard_map/ppermute | solution.py:33
  66.7 44.0 %collective-permute-start.4 = (bf16[4,64,2048]{2,1,0:T(8,128)(2,1)}, bf16[4,64,2048]{2,1,0:T(8,128)(2,1)S(1)}, u32[]{:S(2)}, u32[]{:S(2)}) collective-permute-start(bf16[4,64,2048]{2,1,0:T(8,128)(2,1)} %bitcast_dynamic-update-slice_fusion.17), channel_id=1, source_target_pairs={{0,4},{2,6},{4,0},{6,2},{8,12},{10,14},{12,8},{14,10},{16,20},{18,... | collective-permute-start | bytes 3145736 | tf_op jit(solution)/shard_map/ppermute | solution.py:33
  72.8 46.7 %collective-permute-start.18 = (bf16[4,64,2048]{2,1,0:T(8,128)(2,1)}, bf16[4,64,2048]{2,1,0:T(8,128)(2,1)S(1)}, u32[]{:S(2)}, u32[]{:S(2)}) collective-permute-start(bf16[4,64,2048]{2,1,0:T(8,128)(2,1)} %bitcast_dynamic-update-slice_fusion.9), channel_id=1, source_target_pairs={{0,2},{2,0},{4,6},{6,4},{8,10},{10,8},{12,14},{14,12},{16,18},{18,... | collective-permute-start | bytes 3145736 | tf_op jit(solution)/shard_map/ppermute | solution.py:33
  97.1 36.1 %collective-permute-start.19 = (bf16[4,64,2048]{2,1,0:T(8,128)(2,1)}, bf16[4,64,2048]{2,1,0:T(8,128)(2,1)S(1)}, u32[]{:S(2)}, u32[]{:S(2)}) collective-permute-start(bf16[4,64,2048]{2,1,0:T(8,128)(2,1)} %bitcast_dynamic-update-slice_fusion.9), channel_id=1, source_target_pairs={{0,4},{2,6},{4,0},{6,2},{8,12},{10,14},{12,8},{14,10},{16,20},{18,... | collective-permute-start | bytes 3145736 | tf_op jit(solution)/shard_map/ppermute | solution.py:33
  110.7 33.7 %collective-permute-start.5 = (bf16[4,64,1024]{2,1,0:T(8,128)(2,1)S(1)}, bf16[4,64,1024]{2,1,0:T(8,128)(2,1)S(1)}, u32[]{:S(2)}, u32[]{:S(2)}) collective-permute-start(bf16[4,64,1024]{2,1,0:T(8,128)(2,1)S(1)} %slice.276), channel_id=1, source_target_pairs={{0,4},{2,6},{4,0},{6,2},{8,12},{10,14},{12,8},{14,10},{16,20},{18,... | collective-permute-start | bytes 1572872 | tf_op jit(solution)/shard_map/ppermute | solution.py:33
  112.3 33.6 %collective-permute-start.6 = (bf16[4,64,1024]{2,1,0:T(8,128)(2,1)S(1)}, bf16[4,64,1024]{2,1,0:T(8,128)(2,1)S(1)}, u32[]{:S(2)}, u32[]{:S(2)}) collective-permute-start(bf16[4,64,1024]{2,1,0:T(8,128)(2,1)S(1)} %slice.277), channel_id=1, source_target_pairs={{0,2},{2,0},{4,6},{6,4},{8,10},{10,8},{12,14},{14,12},{16,18},{18,... | collective-permute-start | bytes 1572872 | tf_op jit(solution)/shard_map/ppermute | solution.py:33
  114.9 62.7 %collective-permute-start.13 = (bf16[4,64,1024]{2,1,0:T(8,128)(2,1)}, bf16[4,64,1024]{2,1,0:T(8,128)(2,1)}, u32[]{:S(2)}, u32[]{:S(2)}) collective-permute-start(bf16[4,64,1024]{2,1,0:T(8,128)(2,1)} %slice.283), channel_id=1, source_target_pairs={{0,4},{2,6},{4,0},{6,2},{8,12},{10,14},{12,8},{14,10},{16,20},{18,... | collective-permute-start | bytes 1572872 | tf_op jit(solution)/shard_map/ppermute | solution.py:33
  119.5 58.1 %collective-permute-start.14 = (bf16[4,64,1024]{2,1,0:T(8,128)(2,1)}, bf16[4,64,1024]{2,1,0:T(8,128)(2,1)}, u32[]{:S(2)}, u32[]{:S(2)}) collective-permute-start(bf16[4,64,1024]{2,1,0:T(8,128)(2,1)} %slice.284), channel_id=1, source_target_pairs={{0,2},{2,0},{4,6},{6,4},{8,10},{10,8},{12,14},{14,12},{16,18},{18,... | collective-permute-start | bytes 1572872 | tf_op jit(solution)/shard_map/ppermute | solution.py:33
  133.2 45.7 %collective-permute-start.20 = (bf16[4,64,1024]{2,1,0:T(8,128)(2,1)}, bf16[4,64,1024]{2,1,0:T(8,128)(2,1)}, u32[]{:S(2)}, u32[]{:S(2)}) collective-permute-start(bf16[4,64,1024]{2,1,0:T(8,128)(2,1)} %slice.285), channel_id=1, source_target_pairs={{0,4},{2,6},{4,0},{6,2},{8,12},{10,14},{12,8},{14,10},{16,20},{18,... | collective-permute-start | bytes 1572872 | tf_op jit(solution)/shard_map/ppermute | solution.py:33
  144.4 34.5 %collective-permute-start.21 = (bf16[4,64,1024]{2,1,0:T(8,128)(2,1)}, bf16[4,64,1024]{2,1,0:T(8,128)(2,1)}, u32[]{:S(2)}, u32[]{:S(2)}) collective-permute-start(bf16[4,64,1024]{2,1,0:T(8,128)(2,1)} %slice.286), channel_id=1, source_target_pairs={{0,2},{2,0},{4,6},{6,4},{8,10},{10,8},{12,14},{14,12},{16,18},{18,... | collective-permute-start | bytes 1572872 | tf_op jit(solution)/shard_map/ppermute | solution.py:33
  198.4 28.4 %collective-permute-start.23 = (f32[577,1024]{1,0:T(8,128)}, f32[577,1024]{1,0:T(8,128)}, u32[]{:S(2)}, u32[]{:S(2)}) collective-permute-start(f32[577,1024]{1,0:T(8,128)} %fusion.224), channel_id=1, source_target_pairs={{0,1},{1,0},{2,3},{3,2},{4,5},{5,4},{6,7},{7,6},{8,9},{9,8},{10,11... | collective-permute-start | bytes 7090184 | tf_op jit(solution)/shard_map/ppermute | solution.py:321
  202.1 13.6 %collective-permute-start.32 = (bf16[4,64,1024]{2,1,0:T(8,128)(2,1)}, bf16[4,64,1024]{2,1,0:T(8,128)(2,1)}, u32[]{:S(2)}, u32[]{:S(2)}) collective-permute-start(bf16[4,64,1024]{2,1,0:T(8,128)(2,1)} %get-tuple-element.177), channel_id=1, source_target_pairs={{0,4},{2,6},{4,0},{6,2},{8,12},{10,14},{12,8},{14,10},{16,20},{18,... | collective-permute-start | bytes 1572872 | tf_op jit(solution)/shard_map/ppermute | solution.py:33
  207.7 22.8 %collective-permute-start.22 = (f32[577,1024]{1,0:T(8,128)}, f32[577,1024]{1,0:T(8,128)}, u32[]{:S(2)}, u32[]{:S(2)}) collective-permute-start(f32[577,1024]{1,0:T(8,128)} %fusion.223), channel_id=1, source_target_pairs={{0,1},{1,0},{2,3},{3,2},{4,5},{5,4},{6,7},{7,6},{8,9},{9,8},{10,11... | collective-permute-start | bytes 7090184 | tf_op jit(solution)/shard_map/ppermute | solution.py:321
  210.0 15.0 %collective-permute-start.34 = (bf16[4,64,1024]{2,1,0:T(8,128)(2,1)}, bf16[4,64,1024]{2,1,0:T(8,128)(2,1)S(1)}, u32[]{:S(2)}, u32[]{:S(2)}) collective-permute-start(bf16[4,64,1024]{2,1,0:T(8,128)(2,1)} %get-tuple-element.178), channel_id=1, source_target_pairs={{0,2},{2,0},{4,6},{6,4},{8,10},{10,8},{12,14},{14,12},{16,18},{18,... | collective-permute-start | bytes 1572872 | tf_op jit(solution)/shard_map/ppermute | solution.py:33
  218.0 68.4 %collective-permute-start.33 = (bf16[4,64,2048]{2,1,0:T(8,128)(2,1)}, bf16[4,64,2048]{2,1,0:T(8,128)(2,1)}, u32[]{:S(2)}, u32[]{:S(2)}) collective-permute-start(bf16[4,64,2048]{2,1,0:T(8,128)(2,1)} %pad_maximum_fusion.3), channel_id=1, source_target_pairs={{0,2},{2,0},{4,6},{6,4},{8,10},{10,8},{12,14},{14,12},{16,18},{18,... | collective-permute-start | bytes 3145736 | tf_op jit(solution)/shard_map/ppermute | solution.py:33
  226.3 60.1 %collective-permute-start.35 = (bf16[4,64,2048]{2,1,0:T(8,128)(2,1)}, bf16[4,64,2048]{2,1,0:T(8,128)(2,1)}, u32[]{:S(2)}, u32[]{:S(2)}) collective-permute-start(bf16[4,64,2048]{2,1,0:T(8,128)(2,1)} %pad_maximum_fusion.4), channel_id=1, source_target_pairs={{0,4},{2,6},{4,0},{6,2},{8,12},{10,14},{12,8},{14,10},{16,20},{18,... | collective-permute-start | bytes 3145736 | tf_op jit(solution)/shard_map/ppermute | solution.py:33
  281.2 20.5 %collective-permute-start.24 = (f32[577,1024]{1,0:T(8,128)}, f32[577,1024]{1,0:T(8,128)}, u32[]{:S(2)}, u32[]{:S(2)}) collective-permute-start(f32[577,1024]{1,0:T(8,128)} %convolution_bitcast_fusion), channel_id=1, source_target_pairs={{0,1},{1,0},{2,3},{3,2},{4,5},{5,4},{6,7},{7,6},{8,9},{9,8},{10,11... | collective-permute-start | bytes 7090184 | tf_op jit(solution)/shard_map/ppermute | solution.py:321
  291.2 107.8 %collective-permute-start.36 = (bf16[64,2048]{1,0:T(8,128)(2,1)}, bf16[64,2048]{1,0:T(8,128)(2,1)S(1)}, u32[]{:S(2)}, u32[]{:S(2)}) collective-permute-start(bf16[64,2048]{1,0:T(8,128)(2,1)} %get-tuple-element.174), channel_id=1, source_target_pairs={{0,8},{2,10},{4,12},{6,14},{8,0},{10,2},{12,4},{14,6},{16,24},{18,... | collective-permute-start | bytes 786440 | tf_op jit(solution)/shard_map/ppermute | solution.py:33
  306.6 10.5 %collective-permute-start.46 = (f32[72,128]{1,0:T(8,128)S(1)}, f32[72,128]{1,0:T(8,128)S(1)}, u32[]{:S(2)}, u32[]{:S(2)}) collective-permute-start(f32[72,128]{1,0:T(8,128)S(1)} %constant_dynamic-update-slice_fusion.2), channel_id=1, source_target_pairs={{0,2},{2,0},{4,6},{6,4},{8,10},{10,8},{12,14},{14,12},{16,18},{18,... | collective-permute-start | bytes 110600 | tf_op jit(solution)/shard_map/ppermute | solution.py:33
  324.8 15.1 %collective-permute-start.39 = (bf16[4,64,1024]{2,1,0:T(8,128)(2,1)}, bf16[4,64,1024]{2,1,0:T(8,128)(2,1)}, u32[]{:S(2)}, u32[]{:S(2)}) collective-permute-start(bf16[4,64,1024]{2,1,0:T(8,128)(2,1)} %get-tuple-element.182), channel_id=1, source_target_pairs={{0,4},{2,6},{4,0},{6,2},{8,12},{10,14},{12,8},{14,10},{16,20},{18,... | collective-permute-start | bytes 1572872 | tf_op jit(solution)/shard_map/ppermute | solution.py:33
  326.9 16.9 %collective-permute-start.41 = (bf16[4,64,1024]{2,1,0:T(8,128)(2,1)}, bf16[4,64,1024]{2,1,0:T(8,128)(2,1)}, u32[]{:S(2)}, u32[]{:S(2)}) collective-permute-start(bf16[4,64,1024]{2,1,0:T(8,128)(2,1)} %get-tuple-element.183), channel_id=1, source_target_pairs={{0,2},{2,0},{4,6},{6,4},{8,10},{10,8},{12,14},{14,12},{16,18},{18,... | collective-permute-start | bytes 1572872 | tf_op jit(solution)/shard_map/ppermute | solution.py:33
  328.1 8.5 %collective-permute-start.49 = (f32[72,128]{1,0:T(8,128)S(1)}, f32[72,128]{1,0:T(8,128)S(1)}, u32[]{:S(2)}, u32[]{:S(2)}) collective-permute-start(f32[72,128]{1,0:T(8,128)S(1)} %add.546), channel_id=1, source_target_pairs={{0,16},{2,18},{4,20},{6,22},{8,24},{10,26},{12,28},{14,30},{16,0},... | collective-permute-start | bytes 110600 | tf_op jit(solution)/shard_map/ppermute | solution.py:33
  330.4 20.8 %collective-permute-start.25 = (bf16[4,64,1024]{2,1,0:T(8,128)(2,1)}, bf16[4,64,1024]{2,1,0:T(8,128)(2,1)}, u32[]{:S(2)}, u32[]{:S(2)}) collective-permute-start(bf16[4,64,1024]{2,1,0:T(8,128)(2,1)} %get-tuple-element.187), channel_id=1, source_target_pairs={{0,4},{2,6},{4,0},{6,2},{8,12},{10,14},{12,8},{14,10},{16,20},{18,... | collective-permute-start | bytes 1572872 | tf_op jit(solution)/shard_map/ppermute | solution.py:33
  336.5 17.2 %collective-permute-start.27 = (bf16[4,64,1024]{2,1,0:T(8,128)(2,1)}, bf16[4,64,1024]{2,1,0:T(8,128)(2,1)}, u32[]{:S(2)}, u32[]{:S(2)}) collective-permute-start(bf16[4,64,1024]{2,1,0:T(8,128)(2,1)} %get-tuple-element.188), channel_id=1, source_target_pairs={{0,2},{2,0},{4,6},{6,4},{8,10},{10,8},{12,14},{14,12},{16,18},{18,... | collective-permute-start | bytes 1572872 | tf_op jit(solution)/shard_map/ppermute | solution.py:33
  342.6 32.0 %collective-permute-start.40 = (bf16[4,64,2048]{2,1,0:T(8,128)(2,1)S(1)}, bf16[4,64,2048]{2,1,0:T(8,128)(2,1)S(1)}, u32[]{:S(2)}, u32[]{:S(2)}) collective-permute-start(bf16[4,64,2048]{2,1,0:T(8,128)(2,1)S(1)} %pad_maximum_fusion.5), channel_id=1, source_target_pairs={{0,2},{2,0},{4,6},{6,4},{8,10},{10,8},{12,14},{14,12},{16,18},{18,... | collective-permute-start | bytes 3145736 | tf_op jit(solution)/shard_map/ppermute | solution.py:33
  345.2 31.6 %collective-permute-start.42 = (bf16[4,64,2048]{2,1,0:T(8,128)(2,1)S(1)}, bf16[4,64,2048]{2,1,0:T(8,128)(2,1)S(1)}, u32[]{:S(2)}, u32[]{:S(2)}) collective-permute-start(bf16[4,64,2048]{2,1,0:T(8,128)(2,1)S(1)} %pad_maximum_fusion.6), channel_id=1, source_target_pairs={{0,4},{2,6},{4,0},{6,2},{8,12},{10,14},{12,8},{14,10},{16,20},{18,... | collective-permute-start | bytes 3145736 | tf_op jit(solution)/shard_map/ppermute | solution.py:33
  352.5 43.0 %collective-permute-start.26 = (bf16[4,64,2048]{2,1,0:T(8,128)(2,1)S(1)}, bf16[4,64,2048]{2,1,0:T(8,128)(2,1)S(1)}, u32[]{:S(2)}, u32[]{:S(2)}) collective-permute-start(bf16[4,64,2048]{2,1,0:T(8,128)(2,1)S(1)} %pad_maximum_fusion.1), channel_id=1, source_target_pairs={{0,2},{2,0},{4,6},{6,4},{8,10},{10,8},{12,14},{14,12},{16,18},{18,... | collective-permute-start | bytes 3145736 | tf_op jit(solution)/shard_map/ppermute | solution.py:33
  355.1 41.0 %collective-permute-start.28 = (bf16[4,64,2048]{2,1,0:T(8,128)(2,1)S(1)}, bf16[4,64,2048]{2,1,0:T(8,128)(2,1)S(1)}, u32[]{:S(2)}, u32[]{:S(2)}) collective-permute-start(bf16[4,64,2048]{2,1,0:T(8,128)(2,1)S(1)} %pad_maximum_fusion.2), channel_id=1, source_target_pairs={{0,4},{2,6},{4,0},{6,2},{8,12},{10,14},{12,8},{14,10},{16,20},{18,... | collective-permute-start | bytes 3145736 | tf_op jit(solution)/shard_map/ppermute | solution.py:33
  374.5 30.8 %collective-permute-start.37 = (bf16[64,2048]{1,0:T(8,128)(2,1)}, bf16[64,2048]{1,0:T(8,128)(2,1)}, u32[]{:S(2)}, u32[]{:S(2)}) collective-permute-start(bf16[64,2048]{1,0:T(8,128)(2,1)} %get-tuple-element.176), channel_id=1, source_target_pairs={{0,16},{2,18},{4,20},{6,22},{8,24},{10,26},{12,28},{14,30},{16,0},... | collective-permute-start | bytes 786440 | tf_op jit(solution)/shard_map/ppermute | solution.py:33
  376.8 30.2 %collective-permute-start.38 = (bf16[64,2048]{1,0:T(8,128)(2,1)}, bf16[64,2048]{1,0:T(8,128)(2,1)}, u32[]{:S(2)}, u32[]{:S(2)}) collective-permute-start(bf16[64,2048]{1,0:T(8,128)(2,1)} %get-tuple-element.175), channel_id=1, source_target_pairs={{0,24},{2,26},{4,28},{6,30},{8,16},{10,18},{12,20},{14,22},{16,8},... | collective-permute-start | bytes 786440 | tf_op jit(solution)/shard_map/ppermute | solution.py:33
  395.5 11.9 %collective-permute-start.43 = (bf16[64,2048]{1,0:T(8,128)(2,1)}, bf16[64,2048]{1,0:T(8,128)(2,1)}, u32[]{:S(2)}, u32[]{:S(2)}) collective-permute-start(bf16[64,2048]{1,0:T(8,128)(2,1)} %get-tuple-element.179), channel_id=1, source_target_pairs={{0,8},{2,10},{4,12},{6,14},{8,0},{10,2},{12,4},{14,6},{16,24},{18,... | collective-permute-start | bytes 786440 | tf_op jit(solution)/shard_map/ppermute | solution.py:33
  396.1 17.1 %collective-permute-start.44 = (bf16[64,2048]{1,0:T(8,128)(2,1)}, bf16[64,2048]{1,0:T(8,128)(2,1)}, u32[]{:S(2)}, u32[]{:S(2)}) collective-permute-start(bf16[64,2048]{1,0:T(8,128)(2,1)} %get-tuple-element.181), channel_id=1, source_target_pairs={{0,16},{2,18},{4,20},{6,22},{8,24},{10,26},{12,28},{14,30},{16,0},... | collective-permute-start | bytes 786440 | tf_op jit(solution)/shard_map/ppermute | solution.py:33
  398.9 24.3 %collective-permute-start.45 = (bf16[64,2048]{1,0:T(8,128)(2,1)}, bf16[64,2048]{1,0:T(8,128)(2,1)S(1)}, u32[]{:S(2)}, u32[]{:S(2)}) collective-permute-start(bf16[64,2048]{1,0:T(8,128)(2,1)} %get-tuple-element.180), channel_id=1, source_target_pairs={{0,24},{2,26},{4,28},{6,30},{8,16},{10,18},{12,20},{14,22},{16,8},... | collective-permute-start | bytes 786440 | tf_op jit(solution)/shard_map/ppermute | solution.py:33
  405.4 22.7 %collective-permute-start.29 = (bf16[64,2048]{0,1:T(8,128)(2,1)}, bf16[64,2048]{0,1:T(8,128)(2,1)S(1)}, u32[]{:S(2)}, u32[]{:S(2)}) collective-permute-start(bf16[64,2048]{0,1:T(8,128)(2,1)} %copy.107), channel_id=1, source_target_pairs={{0,8},{2,10},{4,12},{6,14},{8,0},{10,2},{12,4},{14,6},{16,24},{18,... | collective-permute-start | bytes 786440 | tf_op jit(solution)/shard_map/ppermute | solution.py:33
  406.9 46.9 %collective-permute-start.30 = (bf16[64,2048]{0,1:T(8,128)(2,1)}, bf16[64,2048]{0,1:T(8,128)(2,1)S(1)}, u32[]{:S(2)}, u32[]{:S(2)}) collective-permute-start(bf16[64,2048]{0,1:T(8,128)(2,1)} %copy.109), channel_id=1, source_target_pairs={{0,16},{2,18},{4,20},{6,22},{8,24},{10,26},{12,28},{14,30},{16,0},... | collective-permute-start | bytes 786440 | tf_op jit(solution)/shard_map/ppermute | solution.py:33
  407.4 58.2 %collective-permute-start.31 = (bf16[64,2048]{0,1:T(8,128)(2,1)}, bf16[64,2048]{0,1:T(8,128)(2,1)S(1)}, u32[]{:S(2)}, u32[]{:S(2)}) collective-permute-start(bf16[64,2048]{0,1:T(8,128)(2,1)} %copy.110), channel_id=1, source_target_pairs={{0,24},{2,26},{4,28},{6,30},{8,16},{10,18},{12,20},{14,22},{16,8},... | collective-permute-start | bytes 786440 | tf_op jit(solution)/shard_map/ppermute | solution.py:33
  426.9 55.4 %collective-permute-start.58 = (bf16[64,2048]{1,0:T(8,128)(2,1)S(1)}, bf16[64,2048]{1,0:T(8,128)(2,1)S(1)}, u32[]{:S(2)}, u32[]{:S(2)}) collective-permute-start(bf16[64,2048]{1,0:T(8,128)(2,1)S(1)} %get-tuple-element.110), channel_id=1, source_target_pairs={{0,2},{2,0},{4,6},{6,4},{8,10},{10,8},{12,14},{14,12},{16,18},{18,... | collective-permute-start | bytes 786440 | tf_op jit(solution)/shard_map/ppermute | solution.py:33
  478.7 9.2 %collective-permute-start.52 = (bf16[256,512]{0,1:T(8,128)(2,1)S(1)}, bf16[256,512]{0,1:T(8,128)(2,1)S(1)}, u32[]{:S(2)}, u32[]{:S(2)}) collective-permute-start(bf16[256,512]{0,1:T(8,128)(2,1)S(1)} %pad_maximum_fusion.13), channel_id=1, source_target_pairs={{0,8},{2,10},{4,12},{6,14},{8,0},{10,2},{12,4},{14,6},{16,24},{18,... | collective-permute-start | bytes 786440 | tf_op jit(solution)/shard_map/ppermute | solution.py:33
  478.8 17.3 %collective-permute-start.53 = (bf16[256,512]{0,1:T(8,128)(2,1)S(1)}, bf16[256,512]{0,1:T(8,128)(2,1)S(1)}, u32[]{:S(2)}, u32[]{:S(2)}) collective-permute-start(bf16[256,512]{0,1:T(8,128)(2,1)S(1)} %pad_maximum_fusion.13), channel_id=1, source_target_pairs={{0,16},{2,18},{4,20},{6,22},{8,24},{10,26},{12,28},{14,30},{16,0},... | collective-permute-start | bytes 786440 | tf_op jit(solution)/shard_map/ppermute | solution.py:33
  480.1 21.5 %collective-permute-start.54 = (bf16[256,512]{0,1:T(8,128)(2,1)S(1)}, bf16[256,512]{0,1:T(8,128)(2,1)S(1)}, u32[]{:S(2)}, u32[]{:S(2)}) collective-permute-start(bf16[256,512]{0,1:T(8,128)(2,1)S(1)} %pad_maximum_fusion.13), channel_id=1, source_target_pairs={{0,24},{2,26},{4,28},{6,30},{8,16},{10,18},{12,20},{14,22},{16,8},... | collective-permute-start | bytes 786440 | tf_op jit(solution)/shard_map/ppermute | solution.py:33
  483.1 70.6 %collective-permute-start.59 = (bf16[128,2048]{1,0:T(8,128)(2,1)}, bf16[128,2048]{1,0:T(8,128)(2,1)}, u32[]{:S(2)}, u32[]{:S(2)}) collective-permute-start(bf16[128,2048]{1,0:T(8,128)(2,1)} %pad_maximum_fusion.12), channel_id=1, source_target_pairs={{1,5},{2,6},{4,0},{7,3},{9,13},{10,14},{12,8},{15,11},{17,21},{18,... | collective-permute-start | bytes 1572872 | tf_op jit(solution)/shard_map/ppermute | solution.py:112
  555.8 15.1 %collective-permute-start.60 = (bf16[256,2048]{1,0:T(8,128)(2,1)}, bf16[256,2048]{1,0:T(8,128)(2,1)}, u32[]{:S(2)}, u32[]{:S(2)}) collective-permute-start(bf16[256,2048]{1,0:T(8,128)(2,1)} %pad_maximum_fusion.7), channel_id=1, source_target_pairs={{0,8},{5,13},{27,19},{30,22}} | collective-permute-start | bytes 3145736 | tf_op jit(solution)/shard_map/ppermute | solution.py:112
  557.4 15.8 %collective-permute-start.61 = (bf16[256,2048]{1,0:T(8,128)(2,1)}, bf16[256,2048]{1,0:T(8,128)(2,1)}, u32[]{:S(2)}, u32[]{:S(2)}) collective-permute-start(bf16[256,2048]{1,0:T(8,128)(2,1)} %pad_maximum_fusion.7), channel_id=1, source_target_pairs={{3,19},{6,22},{24,8},{29,13}} | collective-permute-start | bytes 3145736 | tf_op jit(solution)/shard_map/ppermute | solution.py:112
  559.1 24.3 %collective-permute-start.62 = (bf16[256,2048]{1,0:T(8,128)(2,1)}, bf16[256,2048]{1,0:T(8,128)(2,1)}, u32[]{:S(2)}, u32[]{:S(2)}) collective-permute-start(bf16[256,2048]{1,0:T(8,128)(2,1)} %pad_maximum_fusion.7), channel_id=1, source_target_pairs={{11,19},{14,22},{16,8},{21,13}} | collective-permute-start | bytes 3145736 | tf_op jit(solution)/shard_map/ppermute | solution.py:112
  595.1 171.1 %collective-permute-start.63 = (bf16[256,2048]{1,0:T(8,128)(2,1)}, bf16[256,2048]{1,0:T(8,128)(2,1)S(1)}, u32[]{:S(2)}, u32[]{:S(2)}) collective-permute-start(bf16[256,2048]{1,0:T(8,128)(2,1)} %get-tuple-element.147), channel_id=1, source_target_pairs={{8,0},{13,5},{19,27},{22,30}} | collective-permute-start | bytes 3145736 | tf_op jit(solution)/shard_map/ppermute | solution.py:112
  596.0 170.3 %collective-permute-start.64 = (bf16[256,2048]{1,0:T(8,128)(2,1)}, bf16[256,2048]{1,0:T(8,128)(2,1)}, u32[]{:S(2)}, u32[]{:S(2)}) collective-permute-start(bf16[256,2048]{1,0:T(8,128)(2,1)} %get-tuple-element.149), channel_id=1, source_target_pairs={{8,24},{13,29},{19,3},{22,6}} | collective-permute-start | bytes 3145736 | tf_op jit(solution)/shard_map/ppermute | solution.py:112
  597.6 176.2 %collective-permute-start.65 = (bf16[256,2048]{1,0:T(8,128)(2,1)}, bf16[256,2048]{1,0:T(8,128)(2,1)}, u32[]{:S(2)}, u32[]{:S(2)}) collective-permute-start(bf16[256,2048]{1,0:T(8,128)(2,1)} %get-tuple-element.148), channel_id=1, source_target_pairs={{8,16},{13,21},{19,11},{22,14}} | collective-permute-start | bytes 3145736 | tf_op jit(solution)/shard_map/ppermute | solution.py:112
  599.8 155.9 %collective-permute-start.55 = (bf16[64,512]{0,1:T(8,128)(2,1)}, bf16[64,512]{0,1:T(8,128)(2,1)}, u32[]{:S(2)}, u32[]{:S(2)}) collective-permute-start(bf16[64,512]{0,1:T(8,128)(2,1)} %get-tuple-element.172), channel_id=1, source_target_pairs={{0,2},{2,0},{4,6},{6,4},{8,10},{10,8},{12,14},{14,12},{16,18},{18,... | collective-permute-start | bytes 196616 | tf_op jit(solution)/shard_map/ppermute | solution.py:33
  600.6 164.3 %collective-permute-start.56 = (bf16[64,512]{0,1:T(8,128)(2,1)}, bf16[64,512]{0,1:T(8,128)(2,1)}, u32[]{:S(2)}, u32[]{:S(2)}) collective-permute-start(bf16[64,512]{0,1:T(8,128)(2,1)} %get-tuple-element.171), channel_id=1, source_target_pairs={{0,4},{2,6},{4,0},{6,2},{8,12},{10,14},{12,8},{14,10},{16,20},{18,... | collective-permute-start | bytes 196616 | tf_op jit(solution)/shard_map/ppermute | solution.py:33
  755.7 9.1 %collective-permute-start.57 = (bf16[64,512]{0,1:T(8,128)(2,1)}, bf16[64,512]{0,1:T(8,128)(2,1)}, u32[]{:S(2)}, u32[]{:S(2)}) collective-permute-start(bf16[64,512]{0,1:T(8,128)(2,1)} %get-tuple-element.170), channel_id=1, source_target_pairs={{0,6},{2,4},{4,2},{6,0},{8,14},{10,12},{12,10},{14,8},{16,22},{18,... | collective-permute-start | bytes 196616 | tf_op jit(solution)/shard_map/ppermute | solution.py:33
  776.0 6.7 collective-permute-start.66
  777.3 6.8 collective-permute-start.67
  778.6 9.3 %collective-permute-start.68 = (bf16[64,2048]{1,0:T(8,128)(2,1)S(1)}, bf16[64,2048]{1,0:T(8,128)(2,1)}, u32[]{:S(2)}, u32[]{:S(2)}) collective-permute-start(bf16[64,2048]{1,0:T(8,128)(2,1)S(1)} %get-tuple-element.166), channel_id=1, source_target_pairs={{0,6},{3,5},{5,3},{6,0},{8,14},{11,13},{13,11},{14,8},{16,22},{19,... | collective-permute-start | bytes 786440 | tf_op jit(solution)/shard_map/ppermute | solution.py:112
  (101 other events, 2368.2 us)

commit v2 on v1

--- a/solution.py
+++ b/solution.py
@@ -1,8 +1,11 @@
+import functools
 import math
 
 import jax
 import jax.numpy as jnp
 from jax import lax
+from jax.experimental import pallas as pl
+from jax.experimental.pallas import tpu as pltpu
 from jax.sharding import PartitionSpec as P
 
 HEAD_DIM = 64
@@ -46,12 +49,15 @@
     return lax.dynamic_index_in_dim(buffer, index, axis, keepdims=False)
 
 
-def gather_rows(shard):
+def gather_rows(shards, after=None):
     count = lax.axis_size("fsdp")
     layers = count // PLANE
     flat, layer = place()
+    shard = jnp.concatenate(shards, axis=1) if len(shards) > 1 else shards[0]
+    if after is not None:
+        shard, _ = lax.optimization_barrier((shard, after))
     rows, cols = shard.shape
-    half = cols // 2
+    half = cols // 256 * 128
     column = jnp.zeros((layers, rows, cols), shard.dtype)
     column = put(column, shard, layer, 0)
     for step in range(1, layers):
@@ -60,44 +66,73 @@
     from_y = swap(column, 2)
     across_x = swap(from_x[:, :, :half], 2)
     across_y = swap(from_y[:, :, half:], 1)
-    whole = jnp.zeros((layers, PLANE, rows, cols), shard.dtype)
-    whole = put(whole, column, flat, 1)
-    whole = put(whole, from_x, flat ^ 1, 1)
-    whole = put(whole, from_y, flat ^ 2, 1)
-    whole = put(whole, jnp.concatenate([across_x, across_y], axis=2), flat ^ 3, 1)
-    return whole.reshape(count * rows, cols)
+    far = jnp.concatenate([across_x, across_y], axis=2)
+    results = []
+    start = 0
+    for item in shards:
+        stop = start + item.shape[1]
+        whole = jnp.zeros((layers, PLANE, rows, item.shape[1]), shard.dtype)
+        whole = put(whole, column[:, :, start:stop], flat, 1)
+        whole = put(whole, from_x[:, :, start:stop], flat ^ 1, 1)
+        whole = put(whole, from_y[:, :, start:stop], flat ^ 2, 1)
+        whole = put(whole, far[:, :, start:stop], flat ^ 3, 1)
+        results.append(whole.reshape(count * rows, item.shape[1]))
+        start = stop
+    return (results, (from_x, from_y))
 
 
 def wide(block):
     return block.astype(jnp.float32)
 
 
-def scatter_sum(partial_sum):
+def join(pieces):
+    return jnp.concatenate(pieces, axis=-1) if len(pieces) > 1 else pieces[0]
+
+
+def scatter_begin(partial_sums):
     count = lax.axis_size("fsdp")
     layers = count // PLANE
-    flat, layer = place()
-    cols = partial_sum.shape[1]
-    rows = partial_sum.shape[0] // count
-    half = cols // 2
-    low = partial_sum.astype(jnp.bfloat16).reshape(layers, PLANE, rows, cols)
-    mine = pick(low, flat, 1)
-    to_x = pick(low, flat ^ 1, 1)
-    to_y = pick(low, flat ^ 2, 1)
-    to_far = pick(low, flat ^ 3, 1)
+    flat, _ = place()
+    rows = partial_sums[0].shape[0] // count
+    lows = [
+        item.astype(jnp.bfloat16).reshape(layers, PLANE, rows, item.shape[1])
+        for item in partial_sums
+    ]
+    mine, to_x, to_y, to_far = [
+        join([pick(item, flat ^ bits, 1) for item in lows]) for bits in range(PLANE)
+    ]
+    half = mine.shape[2] // 256 * 128
     left = swap(to_far[:, :, :half], 1)
     right = swap(to_far[:, :, half:], 2)
+    return (mine, to_x, to_y, left, right)
+
+
+def scatter_middle(state):
+    mine, to_x, to_y, left, right = state
+    half = left.shape[2]
     to_y = jnp.concatenate(
         [(wide(to_y[:, :, :half]) + wide(left)).astype(jnp.bfloat16), to_y[:, :, half:]], axis=2
     )
     to_x = jnp.concatenate(
         [to_x[:, :, :half], (wide(to_x[:, :, half:]) + wide(right)).astype(jnp.bfloat16)], axis=2
     )
-    total = wide(mine) + wide(swap(to_x, 1)) + wide(swap(to_y, 2))
+    return (mine, swap(to_x, 1), swap(to_y, 2))
+
+
+def scatter_end(state):
+    mine, from_x, from_y = state
+    layers = lax.axis_size("fsdp") // PLANE
+    _, layer = place()
+    total = wide(mine) + wide(from_x) + wide(from_y)
     total_low = total.astype(jnp.bfloat16)
     result = pick(total, layer, 0)
     for step in range(1, layers):
         result = result + wide(swap(pick(total_low, layer ^ step, 0), PLANE * step))
     return result
+
+
+def scatter_sum(partial_sums):
+    return scatter_end(scatter_middle(scatter_begin(partial_sums)))
 
 
 def total_everywhere(vector):
@@ -220,22 +255,113 @@
     )
 
 
-def orthogonal(matrix):
-    count = matrix.shape[0]
-    current = matrix.astype(jnp.float32)
-    norm_value = jnp.sqrt(jnp.sum(current * current))
-    current = current / (norm_value + NS_EPS)
-    row = lax.broadcasted_iota(jnp.int32, (count, count), 0)
-    on_diagonal = row == lax.broadcasted_iota(jnp.int32, (count, count), 1)
-    for repeat in range(NS_STEPS):
-        gram = low_dot(current, current, ((1,), (1,)))
-        level = jnp.sum(current * current) / count
-        rest = jnp.where(on_diagonal, gram - level, gram)
-        square = low_dot(rest, rest, ((1,), (0,)))
-        poly = (COEF_B + 2.0 * COEF_C * level) * rest + COEF_C * square
-        keep = COEF_A + COEF_B * level + COEF_C * level * level
-        current = keep * current + low_dot(poly, current, ((1,), (0,)))
-    return current.astype(jnp.bfloat16)
+STRIP = 256
+
+
+def orth_kernel(steps, is_first, is_last, active_ref, block_ref, out_ref, *scratch):
+    low, rest, rest_low, poly = scratch[:4]
+    current = scratch[4] if is_last else out_ref
+    count = block_ref.shape[0]
+    strips = count // STRIP
+
+    def strip(index):
+        return pl.ds(pl.multiple_of(index * STRIP, STRIP), STRIP)
+
+    @pl.when(active_ref[0] > 0)
+    def _():
+        def measure(index, total):
+            piece = block_ref[strip(index), :].astype(jnp.float32)
+            return total + jnp.sum(piece * piece)
+
+        if is_first:
+            squares = lax.fori_loop(0, strips, measure, jnp.float32(0.0))
+            norm = jnp.sqrt(jnp.full((1, 128), squares, jnp.float32)) + NS_EPS
+
+        def scale(index, total):
+            piece = block_ref[strip(index), :].astype(jnp.float32)
+            if is_first:
+                piece = piece / norm[:, :1]
+            current[strip(index), :] = piece
+            low[strip(index), :] = piece.astype(jnp.bfloat16)
+            return total + jnp.sum(piece * piece)
+
+        squares = lax.fori_loop(0, strips, scale, jnp.float32(0.0))
+
+        def step(_, squares):
+            level = squares * (1.0 / count)
+
+            def gram(index, carry):
+                part = low_dot(low[strip(index), :], low[...], ((1,), (1,)))
+                row = lax.broadcasted_iota(jnp.int32, part.shape, 0) + index * STRIP
+                col = lax.broadcasted_iota(jnp.int32, part.shape, 1)
+                part = jnp.where(row == col, part - level, part)
+                rest[strip(index), :] = part
+                rest_low[strip(index), :] = part.astype(jnp.bfloat16)
+                return carry
+
+            lax.fori_loop(0, strips, gram, 0)
+
+            def square(index, carry):
+                part = low_dot(rest_low[strip(index), :], rest_low[...], ((1,), (0,)))
+                part = (COEF_B + 2.0 * COEF_C * level) * rest[strip(index), :] + COEF_C * part
+                poly[strip(index), :] = part.astype(jnp.bfloat16)
+                return carry
+
+            lax.fori_loop(0, strips, square, 0)
+            keep = COEF_A + COEF_B * level + COEF_C * level * level
+
+            def advance(index, total):
+                piece = keep * current[strip(index), :] + low_dot(
+                    poly[strip(index), :], low[...], ((1,), (0,))
+                )
+                current[strip(index), :] = piece
+                return total + jnp.sum(piece * piece)
+
+            squares = lax.fori_loop(0, strips, advance, jnp.float32(0.0))
+
+            def round_low(index, carry):
+                low[strip(index), :] = current[strip(index), :].astype(jnp.bfloat16)
+                return carry
+
+            lax.fori_loop(0, strips, round_low, 0)
+            return squares
+
+        lax.fori_loop(0, steps, step, squares)
+        if is_last:
+
+            def leave(index, carry):
+                out_ref[strip(index), :] = low[strip(index), :]
+                return carry
+
+            lax.fori_loop(0, strips, leave, 0)
+
+
+def orthogonal(matrix, active, steps=NS_STEPS, is_first=True, is_last=True):
+    rows, cols = matrix.shape
+    work = steps * 2 * rows * rows * (2 * cols + rows)
+    scratch = [
+        pltpu.VMEM((rows, cols), jnp.bfloat16),
+        pltpu.VMEM((rows, rows), jnp.float32),
+        pltpu.VMEM((rows, rows), jnp.bfloat16),
+        pltpu.VMEM((rows, rows), jnp.bfloat16),
+    ]
+    if is_last:
+        scratch.append(pltpu.VMEM((rows, cols), jnp.float32))
+    return pl.pallas_call(
+        functools.partial(orth_kernel, steps, is_first, is_last),
+        out_shape=jax.ShapeDtypeStruct((rows, cols), jnp.bfloat16 if is_last else jnp.float32),
+        in_specs=[
+            pl.BlockSpec(memory_space=pltpu.SMEM),
+            pl.BlockSpec(memory_space=pltpu.VMEM),
+        ],
+        out_specs=pl.BlockSpec(memory_space=pltpu.VMEM),
+        scratch_shapes=scratch,
+        compiler_params=pltpu.CompilerParams(vmem_limit_bytes=42 * 1024 * 1024),
+        cost_estimate=pl.CostEstimate(
+            flops=work, bytes_accessed=4 * rows * cols, transcendentals=0
+        ),
+        name="orth",
+    )(active, matrix)
 
 
 def gelu_value(upper):
@@ -345,19 +471,16 @@
 ):
     shard_rows = qkv_weight.shape[0]
     head_width = qkv_weight.shape[2]
-    first = jnp.concatenate([qkv_weight.reshape(shard_rows, -1), out_weight], axis=1)
-    first = gather_rows(first)
-    qkv_full = first[:, : 3 * head_width].reshape(-1, 3, head_width)
-    out_full = first[:, 3 * head_width :]
-    up_full = gather_rows(up_weight)
-    down_full = gather_rows(down_weight)
+    (qkv_full,), mark = gather_rows([qkv_weight.reshape(shard_rows, -1)])
+    (out_full, up_full), mark = gather_rows([out_weight, up_weight], mark)
+    (down_full,), mark = gather_rows([down_weight], mark)
     image_count, length, width = images.shape
     tokens = images.reshape(-1, width).astype(jnp.float32)
     hat_one, inv_one = layer_stats(tokens)
     normed1 = (hat_one * norm_gain[0] + norm_bias[0]).astype(jnp.bfloat16)
-    proj = jnp.einsum("td,djh->tjh", normed1, qkv_full, preferred_element_type=jnp.float32)
+    proj = jnp.dot(normed1, qkv_full, preferred_element_type=jnp.float32)
     bias_three = jnp.stack([attn_bias[0], jnp.zeros_like(attn_bias[0]), attn_bias[1]])
-    proj = (proj + bias_three).astype(jnp.bfloat16)
+    proj = (proj + bias_three.reshape(1, -1)).astype(jnp.bfloat16)
     proj_images = proj.reshape(image_count, length, 3, head_width)
     attended = [attend(proj_images[index]) for index in range(image_count)]
     attn_images = jnp.stack([item[0] for item in attended])
@@ -381,6 +504,7 @@
     upper_grad = (hidden_grad * gelu_slope(upper)).astype(jnp.bfloat16)
     ubias_grad = jnp.sum(upper_grad, axis=0, dtype=jnp.float32)
     upw_grad = jnp.einsum("td,tf->df", normed2, upper_grad, preferred_element_type=jnp.float32)
+    upw_grad, upper_grad = lax.optimization_barrier((upw_grad.astype(jnp.bfloat16), upper_grad))
     normed2_grad = tensor_total(
         jnp.einsum("tf,df->td", upper_grad, up_full, preferred_element_type=jnp.float32)
     )
@@ -390,6 +514,7 @@
     rbias_grad = jnp.stack([jnp.sum(mid_grad, axis=0), jnp.sum(grad_top, axis=0)])
     mid_low = mid_grad.astype(jnp.bfloat16)
     outw_grad = jnp.einsum("td,th->dh", mid_low, attn_rows, preferred_element_type=jnp.float32)
+    outw_grad, mid_low = lax.optimization_barrier((outw_grad.astype(jnp.bfloat16), mid_low))
     attn_grad = jnp.dot(mid_low, out_full, preferred_element_type=jnp.float32).astype(jnp.bfloat16)
     mixed_grads = attn_grad.reshape(image_count, length, head_width)
     proj_grad = jnp.stack(
@@ -399,7 +524,8 @@
         ]
     )
     proj_grad = proj_grad.reshape(-1, 3, head_width)
-    qkv_grad = jnp.einsum("td,tjh->djh", normed1, proj_grad, preferred_element_type=jnp.float32)
+    flat_grad = proj_grad.reshape(-1, 3 * head_width)
+    qkv_grad = jnp.einsum("td,th->dh", normed1, flat_grad, preferred_element_type=jnp.float32)
     abias_grad = jnp.stack(
         [
             jnp.sum(proj_grad[:, 0], axis=0, dtype=jnp.float32),
@@ -407,21 +533,28 @@
         ]
     )
     normed1_grad = tensor_total(
-        jnp.einsum("tjh,djh->td", proj_grad, qkv_full, preferred_element_type=jnp.float32)
+        jnp.einsum("th,dh->td", flat_grad, qkv_full, preferred_element_type=jnp.float32)
     )
     gain_one = jnp.sum(normed1_grad * hat_one, axis=0)
     shift_one = jnp.sum(normed1_grad, axis=0)
     input_grad = mid_grad + norm_back(normed1_grad, hat_one, inv_one, norm_gain[0])
     gain_grad = jnp.stack([gain_one, gain_two])
     nbias_grad = jnp.stack([shift_one, shift_two])
-    down_shard = scatter_sum(downw_grad)
-    up_shard = scatter_sum(upw_grad)
-    first_shard = scatter_sum(
-        jnp.concatenate([qkv_grad.reshape(width, -1), outw_grad], axis=1)
-    )
+    down_shard = scatter_sum([downw_grad])
+    middle_shard = scatter_sum([outw_grad, upw_grad])
+    out_shard = middle_shard[:, :head_width]
+    up_shard = middle_shard[:, head_width:]
+    up_new_moment = MOMENTUM * up_moment + up_shard
+    down_new_moment = MOMENTUM * down_moment + down_shard
+    wide_block = bring_wide(
+        up_new_moment.astype(jnp.bfloat16), down_new_moment.astype(jnp.bfloat16)
+    )
+    owns = jnp.reshape(owner_here(), (1,)).astype(jnp.int32)
+    qkv_shard = scatter_sum([qkv_grad])
+    wide_orth = orthogonal(wide_block, owns)
     grad_shards = (
-        first_shard[:, : 3 * head_width].reshape(shard_rows, 3, head_width),
-        first_shard[:, 3 * head_width :],
+        qkv_shard.reshape(shard_rows, 3, head_width),
+        out_shard,
         up_shard,
         down_shard,
     )
@@ -434,13 +567,11 @@
         lines = item.size // 128
         vector_grads.append(packed[start : start + lines].reshape(item.shape))
         start += lines
-    moment_shards = tuple(
-        (
-            MOMENTUM * stored + gradient
-            for stored, gradient in zip(
-                (qkv_moment, out_moment, up_moment, down_moment), grad_shards
-            )
-        )
+    moment_shards = (
+        MOMENTUM * qkv_moment + grad_shards[0],
+        MOMENTUM * out_moment + out_shard,
+        up_new_moment,
+        down_new_moment,
     )
     shard_low = tuple((stored.astype(jnp.bfloat16) for stored in moment_shards))
     weight_shards = [
@@ -451,14 +582,12 @@
         up_weight,
         down_weight,
     ]
-    wide_block = bring_wide(shard_low[2], shard_low[3])
-    wide_orth = lax.cond(owner_here(), orthogonal, jnp.zeros_like, wide_block)
     up_orth, down_orth = return_wide(wide_orth)
     narrow_block = bring_narrow(
         [shard_low[0][:, 0], shard_low[0][:, 1], shard_low[0][:, 2], shard_low[1]]
     )
     plane_rows = PLANE * shard_rows
-    narrow_orth = orthogonal(narrow_block.T).T[:plane_rows]
+    narrow_orth = orthogonal(narrow_block.T, jnp.ones((1,), jnp.int32))[:, :plane_rows].T
     pieces = return_narrow(narrow_orth) + [up_orth, down_orth]
     updated = []
     for stored, piece in zip(weight_shards, pieces):

time: 803 us -> 589 us (0.73)
  the two profiles are of different devices: /device:TPU:16 before, /device:TPU:0 now
where the time goes in v2:
time: 589 us; the launch traced here: 580 us
  waiting for transfers between devices  273 us (46%)
  starting transfers between devices  96.4 us (16%)
  matrix products  69.5 us (12%)
  local copies, waits for them, and re-layouts  62.3 us (11%)
  other arithmetic  57.3 us (10%)
  Pallas kernels  18 us (3%)
    ppermute x55, waiting for transfers between devices, swap(): return lax.ppermute(block, 'fsdp', xor_pairs(lax.axis_size('fsdp'), bits))  183 us
    ppermute x10, waiting for transfers between devices, send(): return lax.ppermute(block, ('fsdp', 'tensor'), sorted(pairs))  90.8 us
    ppermute x55, starting transfers between devices, swap(): return lax.ppermute(block, 'fsdp', xor_pairs(lax.axis_size('fsdp'), bits))  64.7 us
    ppermute x10, starting transfers between devices, send(): return lax.ppermute(block, ('fsdp', 'tensor'), sorted(pairs))  31.6 us
    unnamed x209, local copies, waits for them, and re-layouts  23.1 us
    pallas_call x2, Pallas kernels, orthogonal(): pl.pallas_call(functools.partial(orth_kernel, steps, is_first, is_last),...  18 us
  transfers between devices with their start and end apart: 69, of which 38 were waited for; matrix products, arithmetic and copies ran while one was open for 20% of the time, Pallas kernels for 3%

profile of v2, /device:TPU:0, one launch (start us, length us, event | category | flops | bytes accessed | tf_op | source)
XLA Modules:
  0.0 580.0 jit_solution(11891174576591261308)
XLA Ops:
  1.8 5.1 collective-permute-start.2
  16.1 3.5 collective-permute-done
  19.6 4.0 collective-permute-done.1
  30.4 11.9 %collective-permute-done.4 = bf16[4,64,1536]{2,1,0:T(8,128)(2,1)S(1)} collective-permute-done((bf16[4,64,1536]{2,1,0:T(8,128)(2,1)S(1)}, bf16[4,64,1536]{2,1,0:T(8,128)(2,1)S(1)}, u32[]{:S(2)}, u32[]{:S(2)}) %collective-permute-start.4) | collective-permute-done | bytes 786464 | tf_op jit(solution)/shard_map/ppermute | solution.py:36
  43.6 2.3 collective-permute-start.9
  51.6 13.4 %collective-permute-done.7 = bf16[64,2560]{1,0:T(8,128)(2,1)S(1)} collective-permute-done((bf16[64,2560]{1,0:T(8,128)(2,1)S(1)}, bf16[64,2560]{1,0:T(8,128)(2,1)S(1)}, u32[]{:S(2)}, u32[]{:S(2)}) %collective-permute-start.7) | collective-permute-done | bytes 327712 | tf_op jit(solution)/shard_map/ppermute | solution.py:36
  65.0 6.0 %collective-permute-done.8 = bf16[64,2560]{1,0:T(8,128)(2,1)S(1)} collective-permute-done((bf16[64,2560]{1,0:T(8,128)(2,1)S(1)}, bf16[64,2560]{1,0:T(8,128)(2,1)S(1)}, u32[]{:S(2)}, u32[]{:S(2)}) %collective-permute-start.8) | collective-permute-done | bytes 327712 | tf_op jit(solution)/shard_map/ppermute | solution.py:36
  78.8 3.5 add_convert_fusion
  82.4 2.7 copy.104
  89.3 2.3 copy-done.2
  91.6 3.1 fusion.40
  94.7 4.3 collective-permute-done.11
  101.4 2.5 collective-permute-start.15
  114.6 4.9 collective-permute-done.16
  123.0 2.2 fusion.97
  127.4 14.5 %collective-permute-done.19 = bf16[4,64,2048]{2,1,0:T(8,128)(2,1)S(1)} collective-permute-done((bf16[4,64,2048]{2,1,0:T(8,128)(2,1)S(1)}, bf16[4,64,2048]{2,1,0:T(8,128)(2,1)S(1)}, u32[]{:S(2)}, u32[]{:S(2)}) %collective-permute-start.19) | collective-permute-done | bytes 1048608 | tf_op jit(solution)/shard_map/ppermute | solution.py:36
  145.2 8.5 %collective-permute-done.21 = bf16[4,64,1024]{2,1,0:T(8,128)(2,1)S(1)} collective-permute-done((bf16[4,64,1024]{2,1,0:T(8,128)(2,1)S(1)}, bf16[4,64,1024]{2,1,0:T(8,128)(2,1)S(1)}, u32[]{:S(2)}, u32[]{:S(2)}) %collective-permute-start.21) | collective-permute-done | bytes 524320 | tf_op jit(solution)/shard_map/ppermute | solution.py:36
  155.1 3.3 multiply_convert_fusion.1
  158.4 3.7 convolution_convert_fusion.1
  162.2 5.3 convert_reduce_fusion
  167.5 4.4 convolution_convert_fusion.2
  171.9 2.4 dynamic-slice_bitcast_fusion.2
  176.8 5.8 fusion.99
  182.7 2.9 collective-permute-done.41
  190.9 4.1 fusion.98
  203.2 6.6 %collective-permute-done.42 = bf16[4,64,2048]{2,1,0:T(8,128)(2,1)} collective-permute-done((bf16[4,64,2048]{2,1,0:T(8,128)(2,1)}, bf16[4,64,2048]{2,1,0:T(8,128)(2,1)}, u32[]{:S(2)}, u32[]{:S(2)}) %collective-permute-start.42) | collective-permute-done | bytes 1048608 | tf_op jit(solution)/shard_map/ppermute | solution.py:36
  209.9 2.2 collective-permute-done.40
  212.1 3.8 fusion.78
  216.8 4.3 multiply_reduce_fusion.2
  221.1 4.2 fusion.77
  231.2 7.6 %fusion.37 = bf16[8,64,577]{2,1,0:T(8,128)(2,1)} fusion(bf16[577,8,64]{0,2,1:T(8,128)(2,1)S(1)} %bitcast.361, f32[8,577,577]{1,2,0:T(8,128)} %copy-done.2, f32[8,577]{1,0:T(8,128)S(1)} %log_add_fusion), kind=kOutput, calls=%fused_computation.71 | convolution fusion | flops 349205024 | bytes 11853888 | tf_op jit(solution)/shard_map/hqk,qhe->khe/dot_general | solution.py:429
  238.9 8.5 %multiply_reduce_fusion = (f32[8,577]{1,0:T(8,128)S(1)}, f32[8,577,577]{1,2,0:T(8,128)}) fusion(f32[8,577,577]{1,2,0:T(8,128)} %copy-done.2, f32[8,577]{1,0:T(8,128)S(1)} %log_add_fusion, bf16[577,8,64]{0,2,1:T(8,128)(2,1)S(1)} %bitcast.362, bf16[577,3,8,64]{0,3,2,1:T(8,128)(2,1)S(1)} %bitcast.357), kind=kOutput, calls=%fused_computation.1 | convolution fusion | flops 351568384 | bytes 22657120 | tf_op jit(solution)/shard_map/qhe,khe->hqk/dot_general | solution.py:426
  247.4 6.2 %multiply_convert_fusion = bf16[8,577,577]{1,2,0:T(8,128)(2,1)S(1)} fusion(f32[8,577,577]{1,2,0:T(8,128)} %get-tuple-element.250, f32[8,577,577]{1,2,0:T(8,128)S(1)} %bitcast.354, f32[8,577]{1,0:T(8,128)S(1)} %get-tuple-element.249, f32[8,577]{1,0:T(8,128)S(1)} %log_add_fusion), kind=kLoop, calls=%fused_computation | loop fusion | flops 13317160 | bytes 26671248 | tf_op jit(solution)/shard_map/convert_element_type | solution.py:432
  254.8 2.7 fusion.36
  263.5 4.1 convolution_convert_fusion
  270.8 3.8 fusion.100
  274.6 10.0 %collective-permute-done.27 = bf16[4,64,768]{2,1,0:T(8,128)(2,1)S(1)} collective-permute-done((bf16[4,64,768]{2,1,0:T(8,128)(2,1)S(1)}, bf16[4,64,768]{2,1,0:T(8,128)(2,1)S(1)}, u32[]{:S(2)}, u32[]{:S(2)}) %collective-permute-start.27) | collective-permute-done | bytes 393248 | tf_op jit(solution)/shard_map/ppermute | solution.py:36
  291.9 13.4 %collective-permute-done.28 = bf16[4,64,1536]{2,1,0:T(8,128)(2,1)S(1)} collective-permute-done((bf16[4,64,1536]{2,1,0:T(8,128)(2,1)S(1)}, bf16[4,64,1536]{2,1,0:T(8,128)(2,1)S(1)}, u32[]{:S(2)}, u32[]{:S(2)}) %collective-permute-start.28) | collective-permute-done | bytes 786464 | tf_op jit(solution)/shard_map/ppermute | solution.py:36
  309.1 2.2 collective-permute-start.31
  313.4 2.4 collective-permute-done.29
  320.1 4.1 collective-permute-done.30
  325.6 2.6 collective-permute-done.35
  328.8 2.3 fusion.80
  332.2 2.1 collective-permute-start.38
  335.8 5.5 collective-permute-done.36
  341.3 2.2 collective-permute-start.44
  343.5 6.5 %collective-permute-done.38 = bf16[64,2560]{1,0:T(8,128)(2,1)S(1)} collective-permute-done((bf16[64,2560]{1,0:T(8,128)(2,1)S(1)}, bf16[64,2560]{1,0:T(8,128)(2,1)S(1)}, u32[]{:S(2)}, u32[]{:S(2)}) %collective-permute-start.38) | collective-permute-done | bytes 327712 | tf_op jit(solution)/shard_map/ppermute | solution.py:36
  349.9 16.8 %collective-permute-done.37 = bf16[64,2560]{1,0:T(8,128)(2,1)S(1)} collective-permute-done((bf16[64,2560]{1,0:T(8,128)(2,1)S(1)}, bf16[64,2560]{1,0:T(8,128)(2,1)S(1)}, u32[]{:S(2)}, u32[]{:S(2)}) %collective-permute-start.37) | collective-permute-done | bytes 327712 | tf_op jit(solution)/shard_map/ppermute | solution.py:36
  366.9 2.6 collective-permute-done.44
  369.5 2.3 broadcast_select_fusion
  375.6 2.3 fusion.26
  378.5 3.7 collective-permute-done.46
  382.8 3.2 fusion.25
  386.0 3.8 copy.127
  390.0 3.9 collective-permute-done.48
  395.8 3.0 collective-permute-done.49
  402.7 2.5 collective-permute-start.54
  407.9 8.4 %collective-permute-done.52 = bf16[256,512]{1,0:T(8,128)(2,1)S(1)} collective-permute-done((bf16[256,512]{1,0:T(8,128)(2,1)S(1)}, bf16[256,512]{1,0:T(8,128)(2,1)S(1)}, u32[]{:S(2)}, u32[]{:S(2)}) %collective-permute-start.52) | collective-permute-done | bytes 262176 | tf_op jit(solution)/shard_map/ppermute | solution.py:36
  417.5 5.4 collective-permute-start.60
  425.2 18.0 %orth.2 = bf16[512,1024]{1,0:T(8,128)(2,1)S(1)} custom-call(s32[1]{0:T(128)} %constant.216.clone.1.active_ref, bf16[512,1024]{1,0:T(8,128)(2,1)S(1)} %copy.123.block_ref), custom_call_target="tpu_custom_call" | custom-call | flops 6710886400 | bytes 2097152 | tf_op jit(solution)/shard_map/orth/pallas_call | solution.py:350
  454.2 5.4 collective-permute-done.57
  460.3 4.3 collective-permute-done.55
  465.6 88.0 %collective-permute-done.63 = bf16[256,2048]{1,0:T(8,128)(2,1)S(1)} collective-permute-done((bf16[256,2048]{1,0:T(8,128)(2,1)}, bf16[256,2048]{1,0:T(8,128)(2,1)S(1)}, u32[]{:S(2)}, u32[]{:S(2)}) %collective-permute-start.63) | collective-permute-done | bytes 1048608 | tf_op jit(solution)/shard_map/ppermute | solution.py:147
  555.7 15.9 %collective-permute-start.68 = (bf16[64,2048]{1,0:T(8,128)(2,1)S(1)}, bf16[64,2048]{1,0:T(8,128)(2,1)S(1)}, u32[]{:S(2)}, u32[]{:S(2)}) collective-permute-start(bf16[64,2048]{1,0:T(8,128)(2,1)S(1)} %get-tuple-element.195), channel_id=1, source_target_pairs={{0,6},{3,5},{5,3},{6,0},{8,14},{11,13},{13,11},{14,8},{16,22},{19,... | collective-permute-start | bytes 786440 | tf_op jit(solution)/shard_map/ppermute | solution.py:147
  (462 shorter events, 153.3 us)
Async XLA Ops:
  1.8 21.9 %collective-permute-start.2 = (bf16[64,1536]{1,0:T(8,128)(2,1)S(1)}, bf16[64,1536]{1,0:T(8,128)(2,1)S(1)}, u32[]{:S(2)}, u32[]{:S(2)}) collective-permute-start(bf16[64,1536]{1,0:T(8,128)(2,1)S(1)} %bitcast.387), channel_id=1, source_target_pairs={{0,24},{2,26},{4,28},{6,30},{8,16},{10,18},{12,20},{14,22},{16,8},... | collective-permute-start | bytes 589832 | tf_op jit(solution)/shard_map/ppermute | solution.py:36
  6.9 16.7 %collective-permute-start.1 = (bf16[64,1536]{1,0:T(8,128)(2,1)S(1)}, bf16[64,1536]{1,0:T(8,128)(2,1)S(1)}, u32[]{:S(2)}, u32[]{:S(2)}) collective-permute-start(bf16[64,1536]{1,0:T(8,128)(2,1)S(1)} %bitcast.388), channel_id=1, source_target_pairs={{0,16},{2,18},{4,20},{6,22},{8,24},{10,26},{12,28},{14,30},{16,0},... | collective-permute-start | bytes 589832 | tf_op jit(solution)/shard_map/ppermute | solution.py:36
  6.9 12.7 %collective-permute-start = (bf16[64,1536]{1,0:T(8,128)(2,1)S(1)}, bf16[64,1536]{1,0:T(8,128)(2,1)S(1)}, u32[]{:S(2)}, u32[]{:S(2)}) collective-permute-start(bf16[64,1536]{1,0:T(8,128)(2,1)S(1)} %bitcast.389), channel_id=1, source_target_pairs={{0,8},{2,10},{4,12},{6,14},{8,0},{10,2},{12,4},{14,6},{16,24},{18,... | collective-permute-start | bytes 589832 | tf_op jit(solution)/shard_map/ppermute | solution.py:36
  23.7 18.7 %collective-permute-start.4 = (bf16[4,64,1536]{2,1,0:T(8,128)(2,1)S(1)}, bf16[4,64,1536]{2,1,0:T(8,128)(2,1)S(1)}, u32[]{:S(2)}, u32[]{:S(2)}) collective-permute-start(bf16[4,64,1536]{2,1,0:T(8,128)(2,1)S(1)} %bitcast_dynamic-update-slice_fusion.14), channel_id=1, source_target_pairs={{0,4},{2,6},{4,0},{6,2},{8,12},{10,14},{12,8},{14,10},{16,20},{18,... | collective-permute-start | bytes 2359304 | tf_op jit(solution)/shard_map/ppermute | solution.py:36
  25.3 18.3 %collective-permute-start.3 = (bf16[4,64,1536]{2,1,0:T(8,128)(2,1)S(1)}, bf16[4,64,1536]{2,1,0:T(8,128)(2,1)S(1)}, u32[]{:S(2)}, u32[]{:S(2)}) collective-permute-start(bf16[4,64,1536]{2,1,0:T(8,128)(2,1)S(1)} %bitcast_dynamic-update-slice_fusion.14), channel_id=1, source_target_pairs={{0,2},{2,0},{4,6},{6,4},{8,10},{10,8},{12,14},{14,12},{16,18},{18,... | collective-permute-start | bytes 2359304 | tf_op jit(solution)/shard_map/ppermute | solution.py:36
  43.6 27.5 %collective-permute-start.9 = (bf16[64,2560]{1,0:T(8,128)(2,1)S(1)}, bf16[64,2560]{1,0:T(8,128)(2,1)S(1)}, u32[]{:S(2)}, u32[]{:S(2)}) collective-permute-start(bf16[64,2560]{1,0:T(8,128)(2,1)S(1)} %copy-done.27), channel_id=1, source_target_pairs={{0,24},{2,26},{4,28},{6,30},{8,16},{10,18},{12,20},{14,22},{16,8},... | collective-permute-start | bytes 983048 | tf_op jit(solution)/shard_map/ppermute | solution.py:36
  45.9 25.1 %collective-permute-start.8 = (bf16[64,2560]{1,0:T(8,128)(2,1)S(1)}, bf16[64,2560]{1,0:T(8,128)(2,1)S(1)}, u32[]{:S(2)}, u32[]{:S(2)}) collective-permute-start(bf16[64,2560]{1,0:T(8,128)(2,1)S(1)} %copy-done.27), channel_id=1, source_target_pairs={{0,16},{2,18},{4,20},{6,22},{8,24},{10,26},{12,28},{14,30},{16,0},... | collective-permute-start | bytes 983048 | tf_op jit(solution)/shard_map/ppermute | solution.py:36
  45.9 19.1 %collective-permute-start.7 = (bf16[64,2560]{1,0:T(8,128)(2,1)S(1)}, bf16[64,2560]{1,0:T(8,128)(2,1)S(1)}, u32[]{:S(2)}, u32[]{:S(2)}) collective-permute-start(bf16[64,2560]{1,0:T(8,128)(2,1)S(1)} %copy-done.27), channel_id=1, source_target_pairs={{0,8},{2,10},{4,12},{6,14},{8,0},{10,2},{12,4},{14,6},{16,24},{18,... | collective-permute-start | bytes 983048 | tf_op jit(solution)/shard_map/ppermute | solution.py:36
  48.0 27.8 %collective-permute-start.6 = (bf16[4,64,768]{2,1,0:T(8,128)(2,1)S(1)}, bf16[4,64,768]{2,1,0:T(8,128)(2,1)S(1)}, u32[]{:S(2)}, u32[]{:S(2)}) collective-permute-start(bf16[4,64,768]{2,1,0:T(8,128)(2,1)S(1)} %slice.300), channel_id=1, source_target_pairs={{0,2},{2,0},{4,6},{6,4},{8,10},{10,8},{12,14},{14,12},{16,18},{18,... | collective-permute-start | bytes 1179656 | tf_op jit(solution)/shard_map/ppermute | solution.py:36
  49.6 26.2 %collective-permute-start.5 = (bf16[4,64,768]{2,1,0:T(8,128)(2,1)S(1)}, bf16[4,64,768]{2,1,0:T(8,128)(2,1)S(1)}, u32[]{:S(2)}, u32[]{:S(2)}) collective-permute-start(bf16[4,64,768]{2,1,0:T(8,128)(2,1)S(1)} %slice.299), channel_id=1, source_target_pairs={{0,4},{2,6},{4,0},{6,2},{8,12},{10,14},{12,8},{14,10},{16,20},{18,... | collective-permute-start | bytes 1179656 | tf_op jit(solution)/shard_map/ppermute | solution.py:36
  71.1 27.9 %collective-permute-start.11 = (bf16[4,64,2560]{2,1,0:T(8,128)(2,1)S(1)}, bf16[4,64,2560]{2,1,0:T(8,128)(2,1)}, u32[]{:S(2)}, u32[]{:S(2)}) collective-permute-start(bf16[4,64,2560]{2,1,0:T(8,128)(2,1)S(1)} %bitcast_dynamic-update-slice_fusion.6), channel_id=1, source_target_pairs={{0,4},{2,6},{4,0},{6,2},{8,12},{10,14},{12,8},{14,10},{16,20},{18,... | collective-permute-start | bytes 3932168 | tf_op jit(solution)/shard_map/ppermute | solution.py:36
  71.8 27.6 %collective-permute-start.10 = (bf16[4,64,2560]{2,1,0:T(8,128)(2,1)S(1)}, bf16[4,64,2560]{2,1,0:T(8,128)(2,1)}, u32[]{:S(2)}, u32[]{:S(2)}) collective-permute-start(bf16[4,64,2560]{2,1,0:T(8,128)(2,1)S(1)} %bitcast_dynamic-update-slice_fusion.6), channel_id=1, source_target_pairs={{0,2},{2,0},{4,6},{6,4},{8,10},{10,8},{12,14},{14,12},{16,18},{18,... | collective-permute-start | bytes 3932168 | tf_op jit(solution)/shard_map/ppermute | solution.py:36
  99.4 20.1 %collective-permute-start.17 = (bf16[64,2048]{1,0:T(8,128)(2,1)S(1)}, bf16[64,2048]{1,0:T(8,128)(2,1)S(1)}, u32[]{:S(2)}, u32[]{:S(2)}) collective-permute-start(bf16[64,2048]{1,0:T(8,128)(2,1)S(1)} %copy-done.31), channel_id=1, source_target_pairs={{0,24},{2,26},{4,28},{6,30},{8,16},{10,18},{12,20},{14,22},{16,8},... | collective-permute-start | bytes 786440 | tf_op jit(solution)/shard_map/ppermute | solution.py:36
  101.3 18.2 %collective-permute-start.16 = (bf16[64,2048]{1,0:T(8,128)(2,1)S(1)}, bf16[64,2048]{1,0:T(8,128)(2,1)S(1)}, u32[]{:S(2)}, u32[]{:S(2)}) collective-permute-start(bf16[64,2048]{1,0:T(8,128)(2,1)S(1)} %copy-done.31), channel_id=1, source_target_pairs={{0,16},{2,18},{4,20},{6,22},{8,24},{10,26},{12,28},{14,30},{16,0},... | collective-permute-start | bytes 786440 | tf_op jit(solution)/shard_map/ppermute | solution.py:36
  101.4 13.2 %collective-permute-start.15 = (bf16[64,2048]{1,0:T(8,128)(2,1)S(1)}, bf16[64,2048]{1,0:T(8,128)(2,1)S(1)}, u32[]{:S(2)}, u32[]{:S(2)}) collective-permute-start(bf16[64,2048]{1,0:T(8,128)(2,1)S(1)} %copy-done.31), channel_id=1, source_target_pairs={{0,8},{2,10},{4,12},{6,14},{8,0},{10,2},{12,4},{14,6},{16,24},{18,... | collective-permute-start | bytes 786440 | tf_op jit(solution)/shard_map/ppermute | solution.py:36
  105.0 22.3 %collective-permute-start.14 = (bf16[4,64,1280]{2,1,0:T(8,128)(2,1)S(1)}, bf16[4,64,1280]{2,1,0:T(8,128)(2,1)S(1)}, u32[]{:S(2)}, u32[]{:S(2)}) collective-permute-start(bf16[4,64,1280]{2,1,0:T(8,128)(2,1)S(1)} %slice.312), channel_id=1, source_target_pairs={{0,2},{2,0},{4,6},{6,4},{8,10},{10,8},{12,14},{14,12},{16,18},{18,... | collective-permute-start | bytes 1966088 | tf_op jit(solution)/shard_map/ppermute | solution.py:36
  107.8 14.5 %collective-permute-start.12 = (bf16[4,64,1280]{2,1,0:T(8,128)(2,1)S(1)}, bf16[4,64,1280]{2,1,0:T(8,128)(2,1)S(1)}, u32[]{:S(2)}, u32[]{:S(2)}) collective-permute-start(bf16[4,64,1280]{2,1,0:T(8,128)(2,1)S(1)} %slice.307), channel_id=1, source_target_pairs={{0,4},{2,6},{4,0},{6,2},{8,12},{10,14},{12,8},{14,10},{16,20},{18,... | collective-permute-start | bytes 1966088 | tf_op jit(solution)/shard_map/ppermute | solution.py:36
  119.6 22.4 %collective-permute-start.19 = (bf16[4,64,2048]{2,1,0:T(8,128)(2,1)S(1)}, bf16[4,64,2048]{2,1,0:T(8,128)(2,1)S(1)}, u32[]{:S(2)}, u32[]{:S(2)}) collective-permute-start(bf16[4,64,2048]{2,1,0:T(8,128)(2,1)S(1)} %bitcast_dynamic-update-slice_fusion.10), channel_id=1, source_target_pairs={{0,4},{2,6},{4,0},{6,2},{8,12},{10,14},{12,8},{14,10},{16,20},{18,... | collective-permute-start | bytes 3145736 | tf_op jit(solution)/shard_map/ppermute | solution.py:36
  120.8 23.4 %collective-permute-start.18 = (bf16[4,64,2048]{2,1,0:T(8,128)(2,1)S(1)}, bf16[4,64,2048]{2,1,0:T(8,128)(2,1)S(1)}, u32[]{:S(2)}, u32[]{:S(2)}) collective-permute-start(bf16[4,64,2048]{2,1,0:T(8,128)(2,1)S(1)} %bitcast_dynamic-update-slice_fusion.10), channel_id=1, source_target_pairs={{0,2},{2,0},{4,6},{6,4},{8,10},{10,8},{12,14},{14,12},{16,18},{18,... | collective-permute-start | bytes 3145736 | tf_op jit(solution)/shard_map/ppermute | solution.py:36
  125.2 28.7 %collective-permute-start.13 = (f32[577,1024]{1,0:T(8,128)S(1)}, f32[577,1024]{1,0:T(8,128)S(1)}, u32[]{:S(2)}, u32[]{:S(2)}) collective-permute-start(f32[577,1024]{1,0:T(8,128)S(1)} %fusion.97), channel_id=1, source_target_pairs={{0,1},{1,0},{2,3},{3,2},{4,5},{5,4},{6,7},{7,6},{8,9},{9,8},{10,11... | collective-permute-start | bytes 7090184 | tf_op jit(solution)/shard_map/ppermute | solution.py:447
  142.0 11.7 %collective-permute-start.21 = (bf16[4,64,1024]{2,1,0:T(8,128)(2,1)S(1)}, bf16[4,64,1024]{2,1,0:T(8,128)(2,1)S(1)}, u32[]{:S(2)}, u32[]{:S(2)}) collective-permute-start(bf16[4,64,1024]{2,1,0:T(8,128)(2,1)S(1)} %slice.314), channel_id=1, source_target_pairs={{0,2},{2,0},{4,6},{6,4},{8,10},{10,8},{12,14},{14,12},{16,18},{18,... | collective-permute-start | bytes 1572872 | tf_op jit(solution)/shard_map/ppermute | solution.py:36
  144.2 9.5 %collective-permute-start.20 = (bf16[4,64,1024]{2,1,0:T(8,128)(2,1)S(1)}, bf16[4,64,1024]{2,1,0:T(8,128)(2,1)S(1)}, u32[]{:S(2)}, u32[]{:S(2)}) collective-permute-start(bf16[4,64,1024]{2,1,0:T(8,128)(2,1)S(1)} %slice.313), channel_id=1, source_target_pairs={{0,4},{2,6},{4,0},{6,2},{8,12},{10,14},{12,8},{14,10},{16,20},{18,... | collective-permute-start | bytes 1572872 | tf_op jit(solution)/shard_map/ppermute | solution.py:36
  174.4 13.9 %collective-permute-start.39 = (bf16[4,64,1024]{2,1,0:T(8,128)(2,1)S(1)}, bf16[4,64,1024]{2,1,0:T(8,128)(2,1)S(1)}, u32[]{:S(2)}, u32[]{:S(2)}) collective-permute-start(bf16[4,64,1024]{2,1,0:T(8,128)(2,1)S(1)} %get-tuple-element.201), channel_id=1, source_target_pairs={{0,4},{2,6},{4,0},{6,2},{8,12},{10,14},{12,8},{14,10},{16,20},{18,... | collective-permute-start | bytes 1572872 | tf_op jit(solution)/shard_map/ppermute | solution.py:36
  175.3 10.3 %collective-permute-start.41 = (bf16[4,64,1024]{2,1,0:T(8,128)(2,1)S(1)}, bf16[4,64,1024]{2,1,0:T(8,128)(2,1)S(1)}, u32[]{:S(2)}, u32[]{:S(2)}) collective-permute-start(bf16[4,64,1024]{2,1,0:T(8,128)(2,1)S(1)} %get-tuple-element.202), channel_id=1, source_target_pairs={{0,2},{2,0},{4,6},{6,4},{8,10},{10,8},{12,14},{14,12},{16,18},{18,... | collective-permute-start | bytes 1572872 | tf_op jit(solution)/shard_map/ppermute | solution.py:36
  182.6 34.2 %collective-permute-start.23 = (f32[577,1024]{1,0:T(8,128)}, f32[577,1024]{1,0:T(8,128)}, u32[]{:S(2)}, u32[]{:S(2)}) collective-permute-start(f32[577,1024]{1,0:T(8,128)} %fusion.99), channel_id=1, source_target_pairs={{0,1},{1,0},{2,3},{3,2},{4,5},{5,4},{6,7},{7,6},{8,9},{9,8},{10,11... | collective-permute-start | bytes 7090184 | tf_op jit(solution)/shard_map/ppermute | solution.py:447
  186.9 23.0 %collective-permute-start.42 = (bf16[4,64,2048]{2,1,0:T(8,128)(2,1)}, bf16[4,64,2048]{2,1,0:T(8,128)(2,1)}, u32[]{:S(2)}, u32[]{:S(2)}) collective-permute-start(bf16[4,64,2048]{2,1,0:T(8,128)(2,1)} %pad_maximum_fusion.4), channel_id=1, source_target_pairs={{0,4},{2,6},{4,0},{6,2},{8,12},{10,14},{12,8},{14,10},{16,20},{18,... | collective-permute-start | bytes 3145736 | tf_op jit(solution)/shard_map/ppermute | solution.py:36
  189.5 22.6 %collective-permute-start.40 = (bf16[4,64,2048]{2,1,0:T(8,128)(2,1)}, bf16[4,64,2048]{2,1,0:T(8,128)(2,1)}, u32[]{:S(2)}, u32[]{:S(2)}) collective-permute-start(bf16[4,64,2048]{2,1,0:T(8,128)(2,1)} %pad_maximum_fusion.3), channel_id=1, source_target_pairs={{0,2},{2,0},{4,6},{6,4},{8,10},{10,8},{12,14},{14,12},{16,18},{18,... | collective-permute-start | bytes 3145736 | tf_op jit(solution)/shard_map/ppermute | solution.py:36
  195.0 26.1 %collective-permute-start.22 = (f32[577,1024]{1,0:T(8,128)}, f32[577,1024]{1,0:T(8,128)}, u32[]{:S(2)}, u32[]{:S(2)}) collective-permute-start(f32[577,1024]{1,0:T(8,128)} %fusion.98), channel_id=1, source_target_pairs={{0,1},{1,0},{2,3},{3,2},{4,5},{5,4},{6,7},{7,6},{8,9},{9,8},{10,11... | collective-permute-start | bytes 7090184 | tf_op jit(solution)/shard_map/ppermute | solution.py:447
  261.7 27.6 %collective-permute-start.32 = (bf16[4,64,1280]{2,1,0:T(8,128)(2,1)S(1)}, bf16[4,64,1280]{2,1,0:T(8,128)(2,1)S(1)}, u32[]{:S(2)}, u32[]{:S(2)}) collective-permute-start(bf16[4,64,1280]{2,1,0:T(8,128)(2,1)S(1)} %get-tuple-element.207), channel_id=1, source_target_pairs={{0,4},{2,6},{4,0},{6,2},{8,12},{10,14},{12,8},{14,10},{16,20},{18,... | collective-permute-start | bytes 1966088 | tf_op jit(solution)/shard_map/ppermute | solution.py:36
  262.5 24.1 %collective-permute-start.34 = (bf16[4,64,1280]{2,1,0:T(8,128)(2,1)S(1)}, bf16[4,64,1280]{2,1,0:T(8,128)(2,1)S(1)}, u32[]{:S(2)}, u32[]{:S(2)}) collective-permute-start(bf16[4,64,1280]{2,1,0:T(8,128)(2,1)S(1)} %get-tuple-element.208), channel_id=1, source_target_pairs={{0,2},{2,0},{4,6},{6,4},{8,10},{10,8},{12,14},{14,12},{16,18},{18,... | collective-permute-start | bytes 1966088 | tf_op jit(solution)/shard_map/ppermute | solution.py:36
  267.9 18.2 %collective-permute-start.25 = (bf16[4,64,768]{2,1,0:T(8,128)(2,1)S(1)}, bf16[4,64,768]{2,1,0:T(8,128)(2,1)S(1)}, u32[]{:S(2)}, u32[]{:S(2)}) collective-permute-start(bf16[4,64,768]{2,1,0:T(8,128)(2,1)S(1)} %get-tuple-element.212), channel_id=1, source_target_pairs={{0,4},{2,6},{4,0},{6,2},{8,12},{10,14},{12,8},{14,10},{16,20},{18,... | collective-permute-start | bytes 1179656 | tf_op jit(solution)/shard_map/ppermute | solution.py:36
  269.1 15.5 %collective-permute-start.27 = (bf16[4,64,768]{2,1,0:T(8,128)(2,1)S(1)}, bf16[4,64,768]{2,1,0:T(8,128)(2,1)S(1)}, u32[]{:S(2)}, u32[]{:S(2)}) collective-permute-start(bf16[4,64,768]{2,1,0:T(8,128)(2,1)S(1)} %get-tuple-element.213), channel_id=1, source_target_pairs={{0,2},{2,0},{4,6},{6,4},{8,10},{10,8},{12,14},{14,12},{16,18},{18,... | collective-permute-start | bytes 1179656 | tf_op jit(solution)/shard_map/ppermute | solution.py:36
  284.8 20.5 %collective-permute-start.28 = (bf16[4,64,1536]{2,1,0:T(8,128)(2,1)S(1)}, bf16[4,64,1536]{2,1,0:T(8,128)(2,1)S(1)}, u32[]{:S(2)}, u32[]{:S(2)}) collective-permute-start(bf16[4,64,1536]{2,1,0:T(8,128)(2,1)S(1)} %pad_maximum_fusion.8), channel_id=1, source_target_pairs={{0,4},{2,6},{4,0},{6,2},{8,12},{10,14},{12,8},{14,10},{16,20},{18,... | collective-permute-start | bytes 2359304 | tf_op jit(solution)/shard_map/ppermute | solution.py:36
  286.3 20.5 %collective-permute-start.26 = (bf16[4,64,1536]{2,1,0:T(8,128)(2,1)S(1)}, bf16[4,64,1536]{2,1,0:T(8,128)(2,1)S(1)}, u32[]{:S(2)}, u32[]{:S(2)}) collective-permute-start(bf16[4,64,1536]{2,1,0:T(8,128)(2,1)S(1)} %pad_maximum_fusion.7), channel_id=1, source_target_pairs={{0,2},{2,0},{4,6},{6,4},{8,10},{10,8},{12,14},{14,12},{16,18},{18,... | collective-permute-start | bytes 2359304 | tf_op jit(solution)/shard_map/ppermute | solution.py:36
  288.5 39.7 %collective-permute-start.35 = (bf16[4,64,2560]{2,1,0:T(8,128)(2,1)}, bf16[4,64,2560]{2,1,0:T(8,128)(2,1)}, u32[]{:S(2)}, u32[]{:S(2)}) collective-permute-start(bf16[4,64,2560]{2,1,0:T(8,128)(2,1)} %pad_maximum_fusion.1), channel_id=1, source_target_pairs={{0,4},{2,6},{4,0},{6,2},{8,12},{10,14},{12,8},{14,10},{16,20},{18,... | collective-permute-start | bytes 3932168 | tf_op jit(solution)/shard_map/ppermute | solution.py:36
  290.7 38.2 %collective-permute-start.33 = (bf16[4,64,2560]{2,1,0:T(8,128)(2,1)}, bf16[4,64,2560]{2,1,0:T(8,128)(2,1)}, u32[]{:S(2)}, u32[]{:S(2)}) collective-permute-start(bf16[4,64,2560]{2,1,0:T(8,128)(2,1)} %fusion.42), channel_id=1, source_target_pairs={{0,2},{2,0},{4,6},{6,4},{8,10},{10,8},{12,14},{14,12},{16,18},{18,... | collective-permute-start | bytes 3932168 | tf_op jit(solution)/shard_map/ppermute | solution.py:36
  309.1 6.7 %collective-permute-start.29 = (bf16[64,1536]{1,0:T(8,128)(2,1)}, bf16[64,1536]{1,0:T(8,128)(2,1)}, u32[]{:S(2)}, u32[]{:S(2)}) collective-permute-start(bf16[64,1536]{1,0:T(8,128)(2,1)} %get-tuple-element.209), channel_id=1, source_target_pairs={{0,8},{2,10},{4,12},{6,14},{8,0},{10,2},{12,4},{14,6},{16,24},{18,... | collective-permute-start | bytes 589832 | tf_op jit(solution)/shard_map/ppermute | solution.py:36
  309.1 8.8 %collective-permute-start.31 = (bf16[64,1536]{1,0:T(8,128)(2,1)}, bf16[64,1536]{1,0:T(8,128)(2,1)}, u32[]{:S(2)}, u32[]{:S(2)}) collective-permute-start(bf16[64,1536]{1,0:T(8,128)(2,1)} %get-tuple-element.210), channel_id=1, source_target_pairs={{0,24},{2,26},{4,28},{6,30},{8,16},{10,18},{12,20},{14,22},{16,8},... | collective-permute-start | bytes 589832 | tf_op jit(solution)/shard_map/ppermute | solution.py:36
  311.3 12.9 %collective-permute-start.30 = (bf16[64,1536]{1,0:T(8,128)(2,1)}, bf16[64,1536]{1,0:T(8,128)(2,1)}, u32[]{:S(2)}, u32[]{:S(2)}) collective-permute-start(bf16[64,1536]{1,0:T(8,128)(2,1)} %get-tuple-element.211), channel_id=1, source_target_pairs={{0,16},{2,18},{4,20},{6,22},{8,24},{10,26},{12,28},{14,30},{16,0},... | collective-permute-start | bytes 589832 | tf_op jit(solution)/shard_map/ppermute | solution.py:36
  315.8 51.0 %collective-permute-start.43 = (bf16[64,2048]{1,0:T(8,128)(2,1)}, bf16[64,2048]{1,0:T(8,128)(2,1)S(1)}, u32[]{:S(2)}, u32[]{:S(2)}) collective-permute-start(bf16[64,2048]{1,0:T(8,128)(2,1)} %get-tuple-element.198), channel_id=1, source_target_pairs={{0,8},{2,10},{4,12},{6,14},{8,0},{10,2},{12,4},{14,6},{16,24},{18,... | collective-permute-start | bytes 786440 | tf_op jit(solution)/shard_map/ppermute | solution.py:36
  318.0 48.9 %collective-permute-start.45 = (bf16[64,2048]{1,0:T(8,128)(2,1)S(1)}, bf16[64,2048]{1,0:T(8,128)(2,1)S(1)}, u32[]{:S(2)}, u32[]{:S(2)}) collective-permute-start(bf16[64,2048]{1,0:T(8,128)(2,1)S(1)} %copy-done.45), channel_id=1, source_target_pairs={{0,24},{2,26},{4,28},{6,30},{8,16},{10,18},{12,20},{14,22},{16,8},... | collective-permute-start | bytes 786440 | tf_op jit(solution)/shard_map/ppermute | solution.py:36
  331.3 10.0 %collective-permute-start.36 = (bf16[64,2560]{1,0:T(8,128)(2,1)S(1)}, bf16[64,2560]{1,0:T(8,128)(2,1)S(1)}, u32[]{:S(2)}, u32[]{:S(2)}) collective-permute-start(bf16[64,2560]{1,0:T(8,128)(2,1)S(1)} %get-tuple-element.188), channel_id=1, source_target_pairs={{0,8},{2,10},{4,12},{6,14},{8,0},{10,2},{12,4},{14,6},{16,24},{18,... | collective-permute-start | bytes 983048 | tf_op jit(solution)/shard_map/ppermute | solution.py:36
  332.2 17.7 %collective-permute-start.38 = (bf16[64,2560]{1,0:T(8,128)(2,1)S(1)}, bf16[64,2560]{1,0:T(8,128)(2,1)S(1)}, u32[]{:S(2)}, u32[]{:S(2)}) collective-permute-start(bf16[64,2560]{1,0:T(8,128)(2,1)S(1)} %get-tuple-element.189), channel_id=1, source_target_pairs={{0,24},{2,26},{4,28},{6,30},{8,16},{10,18},{12,20},{14,22},{16,8},... | collective-permute-start | bytes 983048 | tf_op jit(solution)/shard_map/ppermute | solution.py:36
  334.3 32.4 %collective-permute-start.37 = (bf16[64,2560]{1,0:T(8,128)(2,1)S(1)}, bf16[64,2560]{1,0:T(8,128)(2,1)S(1)}, u32[]{:S(2)}, u32[]{:S(2)}) collective-permute-start(bf16[64,2560]{1,0:T(8,128)(2,1)S(1)} %get-tuple-element.190), channel_id=1, source_target_pairs={{0,16},{2,18},{4,20},{6,22},{8,24},{10,26},{12,28},{14,30},{16,0},... | collective-permute-start | bytes 983048 | tf_op jit(solution)/shard_map/ppermute | solution.py:36
  341.3 28.2 %collective-permute-start.44 = (bf16[64,2048]{1,0:T(8,128)(2,1)S(1)}, bf16[64,2048]{1,0:T(8,128)(2,1)S(1)}, u32[]{:S(2)}, u32[]{:S(2)}) collective-permute-start(bf16[64,2048]{1,0:T(8,128)(2,1)S(1)} %copy-done.44), channel_id=1, source_target_pairs={{0,16},{2,18},{4,20},{6,22},{8,24},{10,26},{12,28},{14,30},{16,0},... | collective-permute-start | bytes 786440 | tf_op jit(solution)/shard_map/ppermute | solution.py:36
  349.9 25.7 %collective-permute-start.24 = (f32[577,1024]{1,0:T(8,128)S(1)}, f32[577,1024]{1,0:T(8,128)S(1)}, u32[]{:S(2)}, u32[]{:S(2)}) collective-permute-start(f32[577,1024]{1,0:T(8,128)S(1)} %copy-done.20), channel_id=1, source_target_pairs={{0,1},{1,0},{2,3},{3,2},{4,5},{5,4},{6,7},{7,6},{8,9},{9,8},{10,11... | collective-permute-start | bytes 7090184 | tf_op jit(solution)/shard_map/ppermute | solution.py:447
  371.8 29.5 %collective-permute-start.58 = (bf16[64,2048]{1,0:T(8,128)(2,1)S(1)}, bf16[64,2048]{1,0:T(8,128)(2,1)S(1)}, u32[]{:S(2)}, u32[]{:S(2)}) collective-permute-start(bf16[64,2048]{1,0:T(8,128)(2,1)S(1)} %get-tuple-element.147), channel_id=1, source_target_pairs={{0,2},{2,0},{4,6},{6,4},{8,10},{10,8},{12,14},{14,12},{16,18},{18,... | collective-permute-start | bytes 786440 | tf_op jit(solution)/shard_map/ppermute | solution.py:36
  373.0 17.0 %collective-permute-start.50 = (bf16[128,512]{1,0:T(8,128)(2,1)S(1)}, bf16[128,512]{1,0:T(8,128)(2,1)S(1)}, u32[]{:S(2)}, u32[]{:S(2)}) collective-permute-start(bf16[128,512]{1,0:T(8,128)(2,1)S(1)} %get-tuple-element.223), channel_id=1, source_target_pairs={{0,2},{2,0},{4,6},{6,4},{8,10},{10,8},{12,14},{14,12},{16,18},{18,... | collective-permute-start | bytes 393224 | tf_op jit(solution)/shard_map/ppermute | solution.py:36
  382.2 7.7 %collective-permute-start.47 = (f32[72,128]{1,0:T(8,128)S(1)}, f32[72,128]{1,0:T(8,128)S(1)}, u32[]{:S(2)}, u32[]{:S(2)}) collective-permute-start(f32[72,128]{1,0:T(8,128)S(1)} %add.392), channel_id=1, source_target_pairs={{0,4},{2,6},{4,0},{6,2},{8,12},{10,14},{12,8},{14,10},{16,20},{18,... | collective-permute-start | bytes 110600 | tf_op jit(solution)/shard_map/ppermute | solution.py:36
  395.2 7.5 %collective-permute-start.51 = (bf16[128,512]{1,0:T(8,128)(2,1)S(1)}, bf16[128,512]{1,0:T(8,128)(2,1)S(1)}, u32[]{:S(2)}, u32[]{:S(2)}) collective-permute-start(bf16[128,512]{1,0:T(8,128)(2,1)S(1)} %get-tuple-element.221), channel_id=1, source_target_pairs={{0,4},{2,6},{4,0},{6,2},{8,12},{10,14},{12,8},{14,10},{16,20},{18,... | collective-permute-start | bytes 393224 | tf_op jit(solution)/shard_map/ppermute | solution.py:36
  401.4 15.0 %collective-permute-start.59 = (bf16[128,2048]{1,0:T(8,128)(2,1)S(1)}, bf16[128,2048]{1,0:T(8,128)(2,1)S(1)}, u32[]{:S(2)}, u32[]{:S(2)}) collective-permute-start(bf16[128,2048]{1,0:T(8,128)(2,1)S(1)} %pad_maximum_fusion.13), channel_id=1, source_target_pairs={{1,5},{2,6},{4,0},{7,3},{9,13},{10,14},{12,8},{15,11},{17,21},{18,... | collective-permute-start | bytes 1572872 | tf_op jit(solution)/shard_map/ppermute | solution.py:147
  402.7 20.2 %collective-permute-start.54 = (bf16[256,512]{1,0:T(8,128)(2,1)S(1)}, bf16[256,512]{1,0:T(8,128)(2,1)S(1)}, u32[]{:S(2)}, u32[]{:S(2)}) collective-permute-start(bf16[256,512]{1,0:T(8,128)(2,1)S(1)} %pad_maximum_fusion.15), channel_id=1, source_target_pairs={{0,24},{2,26},{4,28},{6,30},{8,16},{10,18},{12,20},{14,22},{16,8},... | collective-permute-start | bytes 786440 | tf_op jit(solution)/shard_map/ppermute | solution.py:36
  405.2 17.7 %collective-permute-start.53 = (bf16[256,512]{1,0:T(8,128)(2,1)S(1)}, bf16[256,512]{1,0:T(8,128)(2,1)S(1)}, u32[]{:S(2)}, u32[]{:S(2)}) collective-permute-start(bf16[256,512]{1,0:T(8,128)(2,1)S(1)} %pad_maximum_fusion.15), channel_id=1, source_target_pairs={{0,16},{2,18},{4,20},{6,22},{8,24},{10,26},{12,28},{14,30},{16,0},... | collective-permute-start | bytes 786440 | tf_op jit(solution)/shard_map/ppermute | solution.py:36
  405.2 11.1 %collective-permute-start.52 = (bf16[256,512]{1,0:T(8,128)(2,1)S(1)}, bf16[256,512]{1,0:T(8,128)(2,1)S(1)}, u32[]{:S(2)}, u32[]{:S(2)}) collective-permute-start(bf16[256,512]{1,0:T(8,128)(2,1)S(1)} %pad_maximum_fusion.15), channel_id=1, source_target_pairs={{0,8},{2,10},{4,12},{6,14},{8,0},{10,2},{12,4},{14,6},{16,24},{18,... | collective-permute-start | bytes 786440 | tf_op jit(solution)/shard_map/ppermute | solution.py:36
  417.5 25.8 %collective-permute-start.60 = (bf16[256,2048]{1,0:T(8,128)(2,1)}, bf16[256,2048]{1,0:T(8,128)(2,1)}, u32[]{:S(2)}, u32[]{:S(2)}) collective-permute-start(bf16[256,2048]{1,0:T(8,128)(2,1)} %pad_maximum_fusion.5), channel_id=1, source_target_pairs={{0,8},{5,13},{27,19},{30,22}} | collective-permute-start | bytes 3145736 | tf_op jit(solution)/shard_map/ppermute | solution.py:147
  423.5 21.2 %collective-permute-start.62 = (bf16[256,2048]{1,0:T(8,128)(2,1)}, bf16[256,2048]{1,0:T(8,128)(2,1)S(1)}, u32[]{:S(2)}, u32[]{:S(2)}) collective-permute-start(bf16[256,2048]{1,0:T(8,128)(2,1)} %pad_maximum_fusion.5), channel_id=1, source_target_pairs={{11,19},{14,22},{16,8},{21,13}} | collective-permute-start | bytes 3145736 | tf_op jit(solution)/shard_map/ppermute | solution.py:147
  424.4 20.2 %collective-permute-start.61 = (bf16[256,2048]{1,0:T(8,128)(2,1)}, bf16[256,2048]{1,0:T(8,128)(2,1)S(1)}, u32[]{:S(2)}, u32[]{:S(2)}) collective-permute-start(bf16[256,2048]{1,0:T(8,128)(2,1)} %pad_maximum_fusion.5), channel_id=1, source_target_pairs={{3,19},{6,22},{24,8},{29,13}} | collective-permute-start | bytes 3145736 | tf_op jit(solution)/shard_map/ppermute | solution.py:147
  447.6 105.9 %collective-permute-start.63 = (bf16[256,2048]{1,0:T(8,128)(2,1)}, bf16[256,2048]{1,0:T(8,128)(2,1)S(1)}, u32[]{:S(2)}, u32[]{:S(2)}) collective-permute-start(bf16[256,2048]{1,0:T(8,128)(2,1)} %get-tuple-element.174), channel_id=1, source_target_pairs={{8,0},{13,5},{19,27},{22,30}} | collective-permute-start | bytes 3145736 | tf_op jit(solution)/shard_map/ppermute | solution.py:147
  449.1 104.5 %collective-permute-start.65 = (bf16[256,2048]{1,0:T(8,128)(2,1)}, bf16[256,2048]{1,0:T(8,128)(2,1)}, u32[]{:S(2)}, u32[]{:S(2)}) collective-permute-start(bf16[256,2048]{1,0:T(8,128)(2,1)} %get-tuple-element.175), channel_id=1, source_target_pairs={{8,16},{13,21},{19,11},{22,14}} | collective-permute-start | bytes 3145736 | tf_op jit(solution)/shard_map/ppermute | solution.py:147
  450.7 102.8 %collective-permute-start.64 = (bf16[256,2048]{1,0:T(8,128)(2,1)S(1)}, bf16[256,2048]{1,0:T(8,128)(2,1)}, u32[]{:S(2)}, u32[]{:S(2)}) collective-permute-start(bf16[256,2048]{1,0:T(8,128)(2,1)S(1)} %get-tuple-element.176), channel_id=1, source_target_pairs={{8,24},{13,29},{19,3},{22,6}} | collective-permute-start | bytes 3145736 | tf_op jit(solution)/shard_map/ppermute | solution.py:147
  452.6 7.1 %collective-permute-start.57 = (bf16[64,512]{0,1:T(8,128)(2,1)S(1)}, bf16[64,512]{0,1:T(8,128)(2,1)S(1)}, u32[]{:S(2)}, u32[]{:S(2)}) collective-permute-start(bf16[64,512]{0,1:T(8,128)(2,1)S(1)} %get-tuple-element.218), channel_id=1, source_target_pairs={{0,6},{2,4},{4,2},{6,0},{8,14},{10,12},{12,10},{14,8},{16,22},{18,... | collective-permute-start | bytes 196616 | tf_op jit(solution)/shard_map/ppermute | solution.py:36
  453.9 6.4 %collective-permute-start.56 = (bf16[64,512]{0,1:T(8,128)(2,1)S(1)}, bf16[64,512]{0,1:T(8,128)(2,1)S(1)}, u32[]{:S(2)}, u32[]{:S(2)}) collective-permute-start(bf16[64,512]{0,1:T(8,128)(2,1)S(1)} %get-tuple-element.219), channel_id=1, source_target_pairs={{0,4},{2,6},{4,0},{6,2},{8,12},{10,14},{12,8},{14,10},{16,20},{18,... | collective-permute-start | bytes 196616 | tf_op jit(solution)/shard_map/ppermute | solution.py:36
  555.7 20.2 %collective-permute-start.68 = (bf16[64,2048]{1,0:T(8,128)(2,1)S(1)}, bf16[64,2048]{1,0:T(8,128)(2,1)S(1)}, u32[]{:S(2)}, u32[]{:S(2)}) collective-permute-start(bf16[64,2048]{1,0:T(8,128)(2,1)S(1)} %get-tuple-element.195), channel_id=1, source_target_pairs={{0,6},{3,5},{5,3},{6,0},{8,14},{11,13},{13,11},{14,8},{16,22},{19,... | collective-permute-start | bytes 786440 | tf_op jit(solution)/shard_map/ppermute | solution.py:147
  572.9 5.4 collective-permute-start.66
  (101 other events, 1212.4 us)
